TPU v7x, 256 devices: a whole 4x4x8 slice. The times are simulated.
256 devices in a mesh: outer: 32 (over z, x), inner: 8 (over y, core).
Axes of the slice: x: 4, y: 4, z: 8, core: 2. Of those that a mesh axis runs over, the one named last changes fastest.
Arguments:
- query: bfloat16 [32768, 32, 128], P(('outer', 'inner')), may hold values from -6 to 6
- keys: bfloat16 [32768, 32, 128], P(('outer', 'inner')), may hold values from -6 to 6
- value: bfloat16 [32768, 32, 128], P(('outer', 'inner')), may hold values from -6 to 6
- beta: bfloat16 [32768, 32], P(('outer', 'inner')), may hold values from 0 to 1, as said below
Outputs:
- mixed: bfloat16 [32768, 32, 128], P(('outer', 'inner'))
Inputs may be any that keep to these rules, and one draw needn't show every extreme that they name: `beta`: each gate lies strictly between 0 and 1.
All inputs are finite; a program needn't handle non-finite values.
Results may differ from a plain program's by a relative error of at most 0.001.
Values may be sent and summed in bfloat16 or wider, within the bound.
No kernel may reach another device: no remote copies, remote signals or barrier semaphores. Data moves between devices by JAX's collectives and lax.ppermute only.
A program may use at most 128 MiB of HBM per device.

v0:
```python
import jax
import jax.numpy as jnp
from jax import lax
from jax.sharding import PartitionSpec as P

SPAN = 128


HIGH = lax.Precision.HIGHEST


def prefix(x, axis, combine, identity):
    peers, index = (lax.axis_size(axis), lax.axis_index(axis))
    everything = jax.tree.map(lambda part: lax.all_gather(part, axis), x)
    start = jax.tree.map(
        lambda part, zero: jnp.broadcast_to(jnp.asarray(zero, part.dtype), part.shape), x, identity
    )

    def step(k, before):
        reached = k < index
        new = combine(before, jax.tree.map(lambda part: part[k], everything))
        return jax.tree.map(lambda a, b: jnp.where(reached, a, b), new, before)

    return lax.fori_loop(0, peers, step, start)


def unit_rows(block):
    return block * lax.rsqrt(jnp.sum(block * block, axis=-1, keepdims=True) + 1e-06)


def unit_lower_inverse(strict_part):
    size = strict_part.shape[0]
    inverse = jnp.eye(size, dtype=jnp.float32) - strict_part
    power = jnp.dot(strict_part, strict_part, precision=HIGH)
    for level in range((size - 1).bit_length() - 1):
        inverse = inverse + jnp.dot(inverse, power, precision=HIGH)
        power = jnp.dot(power, power, precision=HIGH)
    return inverse


def span_terms(query_block, keys_c, value_c, beta_c):
    width = keys_c.shape[1]
    query_block = query_block.astype(jnp.float32)
    keys_c = keys_c.astype(jnp.float32)
    value_c = value_c.astype(jnp.float32)
    beta_c = beta_c.astype(jnp.float32)
    qnorm = unit_rows(query_block)
    knorm = unit_rows(keys_c)
    kbeta = knorm * beta_c[:, None]
    vbeta = value_c * beta_c[:, None]
    gram = jnp.dot(kbeta, knorm.T, precision=HIGH)
    inverse = unit_lower_inverse(jnp.tril(gram, -1))
    solved = jnp.dot(inverse, jnp.concatenate([kbeta, vbeta], axis=1), precision=HIGH)
    weights = solved[:, :width]
    updates = solved[:, width:]
    scores = jnp.tril(jnp.dot(qnorm, knorm.T, precision=HIGH))
    return (qnorm, knorm, weights, updates, scores)


def combine_pairs(earlier, later):
    trans_a, offset_a = earlier
    trans_b, offset_b = later
    merged = jnp.einsum("hij,hjk->hik", trans_b, trans_a, precision=HIGH)
    shifted = jnp.einsum("hij,hjk->hik", trans_b, offset_a, precision=HIGH) + offset_b
    return (merged, shifted)


def shards(query, keys, value, beta):
    qhead, khead, vhead, bhead = (
        lax.all_to_all(query, "inner", split_axis=1, concat_axis=0, tiled=True),
        lax.all_to_all(keys, "inner", split_axis=1, concat_axis=0, tiled=True),
        lax.all_to_all(value, "inner", split_axis=1, concat_axis=0, tiled=True),
        lax.all_to_all(beta, "inner", split_axis=1, concat_axis=0, tiled=True),
    )
    length, groups, width = qhead.shape
    count = length // SPAN

    def blocks(array):
        return jnp.transpose(array.reshape(count, SPAN, groups, width), (0, 2, 1, 3))

    bblk = jnp.transpose(bhead.reshape(count, SPAN, groups), (0, 2, 1))
    terms_fn = jax.vmap(jax.vmap(span_terms))
    qnorm, knorm, weights, updates, scores = terms_fn(
        blocks(qhead), blocks(khead), blocks(vhead), bblk
    )
    eye = jnp.broadcast_to(jnp.eye(width, dtype=jnp.float32), (groups, width, width))
    zeros = jnp.zeros((groups, width, width), jnp.float32)
    joined_parts = jnp.concatenate([eye, zeros], axis=2)

    def pair_step(carried, kpart, wpart, upart):
        product = jnp.einsum("hcd,hde->hce", wpart, carried, precision=HIGH)
        change = jnp.concatenate([-product[..., :width], upart - product[..., width:]], axis=2)
        nextpair = carried + jnp.einsum("hcd,hce->hde", kpart, change, precision=HIGH)
        return (nextpair, change)

    def transition_only(carried, inputs):
        kpart, wpart, upart = inputs
        nextpair, change = pair_step(carried, kpart, wpart, upart)
        return (nextpair, None)

    final_pair, _ = lax.scan(transition_only, joined_parts, (knorm, weights, updates))
    block_trans = final_pair[..., :width]
    block_offset = final_pair[..., width:]
    _, incoming = prefix((block_trans, block_offset), "outer", combine_pairs, (eye, zeros))

    def advance(state, inputs):
        qpart, kpart, wpart, upart, spart = inputs
        delta = upart - jnp.einsum("hcd,hde->hce", wpart, state, precision=HIGH)
        result = jnp.einsum("hcd,hde->hce", qpart, state, precision=HIGH) + jnp.einsum(
            "hcs,hse->hce", spart, delta, precision=HIGH
        )
        state = state + jnp.einsum("hcd,hce->hde", kpart, delta, precision=HIGH)
        return (state, result.astype(jnp.bfloat16))

    _, outputs = lax.scan(advance, incoming, (qnorm, knorm, weights, updates, scores))
    token_major = jnp.transpose(outputs, (0, 2, 1, 3)).reshape(length, groups, width)
    return lax.all_to_all(token_major, "inner", split_axis=0, concat_axis=1, tiled=True)


def solution(mesh):
    placed = (
        P(("outer", "inner"), None, None),
        P(("outer", "inner"), None, None),
        P(("outer", "inner"), None, None),
        P(("outer", "inner"), None),
    )
    return jax.shard_map(
        shards,
        mesh=mesh,
        in_specs=placed,
        out_specs=P(("outer", "inner"), None, None),
        check_vma=False,
    )
```

profile of v0, /device:TPU:1, one launch (start us, length us, event | category | flops | bytes accessed | tf_op | source)
XLA Modules:
  0.0 445.4 jit_solution(17959281910144616222)
XLA Ops:
  6.5 6.5 %all-to-all-start.1 = ((bf16[128,8,4]{0,2,1:T(4,128)(2,1)}), bf16[128,8,4]{0,2,1:T(4,128)(2,1)S(1)}, u32[]{:S(2)}, u32[]{:S(2)}) async-start(bf16[128,8,4]{0,2,1:T(4,128)(2,1)} %bitcast.145), calls=%async_computation.1 | async-start | bytes 16384 | tf_op jit(solution)/shard_map/all_to_all | solution.py:73
  13.0 2.7 copy.24
  15.7 1.9 all-to-all-done.1
  17.6 4.2 all-to-all-start
  23.4 13.5 %all-to-all-done = bf16[128,32,128]{2,0,1:T(8,128)(2,1)S(1)} async-done(((bf16[128,32,128]{2,0,1:T(8,128)(2,1)}), bf16[128,32,128]{2,0,1:T(8,128)(2,1)S(1)}, u32[]{:S(2)}, u32[]{:S(2)}) %all-to-all-start) | async-done | bytes 1048608 | tf_op jit(solution)/shard_map/all_to_all | solution.py:71
  36.9 4.3 all-to-all-start.2
  41.9 6.5 %fusion.57 = f32[8,4,128,128]{3,2,1,0:T(8,128)S(1)} fusion(bf16[128,8,4,128]{3,0,2,1:T(8,128)(2,1)S(1)} %bitcast.135, f32[8,4,128]{2,1,0:T(4,128)S(1)} %add_rsqrt_fusion.1, f32[8,4,128]{2,1,0:T(4,128)S(1)} %convert_bitcast_fusion.3), kind=kOutput, calls=%fused_computation.68 | convolution fusion | flops 807927808 | bytes 3178496 | tf_op jit(solution)/shard_map/vmap(vmap())/dot_general | solution.py:51
  48.4 2.2 fusion.51
  50.6 2.5 subtract_add_fusion
  53.0 2.0 fusion.75
  55.1 2.0 fusion.77
  57.1 2.2 fusion.76
  59.3 2.2 fusion.78
  61.5 2.3 convolution_add_fusion.5
  63.8 2.0 fusion.80
  65.8 2.2 fusion.79
  68.0 2.0 fusion.81
  70.1 2.5 convolution_add_fusion.4
  73.9 3.5 fusion.82
  77.4 2.2 fusion.59
  80.4 4.3 fusion.35
  84.7 2.6 fusion.73
  87.3 2.9 copy.26
  90.2 33.9 %while.36 = (s32[]{:T(128)}, f32[4,128,256]{2,1,0:T(8,128)S(1)}, f32[8,4,128,128]{2,3,1,0:T(8,128)}, f32[8,4,128,128]{3,2,1,0:T(8,128)}, f32[8,4,128,128]{3,2,1,0:T(8,128)}, /*index=5*/s32[]{:T(128)}) while((s32[]{:T(128)}, f32[4,128,256]{2,1,0:T(8,128)S(1)}, f32[8,4,128,128]{2,3,1,0:T(8,128)}, f32[8,4,128,128]{3,2,1,0:T(8,128)}, ...), condition=%wide.region_2.3_spmd, body=%wide.region_1.0_spmd.sunk | while | flops 403046400 | bytes 4457545 | solution.py:101
  90.2 1.5 fusion.129
  92.8 1.7 convolution_add_fusion.8
  94.4 1.5 fusion.129
  97.0 1.7 convolution_add_fusion.8
  98.7 1.5 fusion.129
  101.2 1.7 convolution_add_fusion.8
  102.9 1.5 fusion.129
  105.5 1.7 convolution_add_fusion.8
  107.2 1.5 fusion.129
  109.7 1.7 convolution_add_fusion.8
  111.4 1.5 fusion.129
  114.0 1.7 convolution_add_fusion.8
  115.7 1.5 fusion.129
  118.2 1.7 convolution_add_fusion.8
  119.9 1.5 fusion.129
  122.5 1.7 convolution_add_fusion.8
  127.2 5.1 %all-to-all-start.3 = ((bf16[128,32,128]{2,0,1:T(8,128)(2,1)}), bf16[128,32,128]{2,0,1:T(8,128)(2,1)S(1)}, u32[]{:S(2)}, u32[]{:S(2)}) async-start(bf16[128,32,128]{2,0,1:T(8,128)(2,1)} %copy.27), calls=%async_computation.3 | async-start | bytes 2097152 | tf_op jit(solution)/shard_map/all_to_all | solution.py:70
  132.3 15.0 %all-to-all-done.3 = bf16[128,32,128]{2,0,1:T(8,128)(2,1)S(1)} async-done(((bf16[128,32,128]{2,0,1:T(8,128)(2,1)}), bf16[128,32,128]{2,0,1:T(8,128)(2,1)S(1)}, u32[]{:S(2)}, u32[]{:S(2)}) %all-to-all-start.3) | async-done | bytes 1048608 | tf_op jit(solution)/shard_map/all_to_all | solution.py:70
  148.0 2.0 fusion.40
  149.9 6.2 %convolution_select_fusion = f32[8,4,128,128]{3,2,1,0:T(8,128)} fusion(bf16[128,8,4,128]{3,0,2,1:T(8,128)(2,1)S(1)} %bitcast.136, f32[8,4,128]{2,1,0:T(4,128)S(1)} %add_rsqrt_fusion.1, pred[128,128]{1,0:T(8,128)(4,1)S(1)} %iota_compare_fusion, bf16[128,8,4,128]{3,0,2,1:T(8,128)(2,1)S(1)} %bitcast.138, f32[8,4,128]{2,1,0:T(4,128)S(1)} %add_rsqrt_fusion), kind=kOutput, calls=%fused_computation.67 | convolution fusion | flops 807927808 | bytes 4243456 | tf_op jit(solution)/shard_map/vmap(vmap())/dot_general | solution.py:56
  156.1 69.1 %all-gather.5.cloned.1.call-done = f32[128,128,128]{2,1,0:T(8,128)} async-done(((f32[4,128,128]{2,1,0:T(8,128)}), f32[128,128,128]{2,1,0:T(8,128)}) %all-gather.5.cloned.1.call-update) | async-done | bytes 8388624 | tf_op jit(solution)/shard_map/all_gather | solution.py:14
  225.2 98.0 %all-gather.7.cloned.1.call-done = f32[128,128,128]{2,1,0:T(8,128)} async-done(((f32[4,128,128]{2,1,0:T(8,128)}), f32[128,128,128]{2,1,0:T(8,128)}) %all-gather.7.cloned.1.call-update) | async-done | bytes 8388624 | tf_op jit(solution)/shard_map/all_gather | solution.py:14
  323.2 47.4 %while.38 = (s32[]{:T(128)}, f32[4,128,128]{2,1,0:T(8,128)S(1)}, s32[]{:T(128)}, f32[32,4,128,128]{3,2,1,0:T(8,128)}, f32[32,4,128,128]{3,2,1,0:T(8,128)}, /*index=5*/s32[]{:T(128)}, s32[]{:T(128)}) while((s32[]{:T(128)}, f32[4,128,128]{2,1,0:T(8,128)S(1)}, s32[]{:T(128)}, f32[32,4,128,128]{3,2,1,0:T(8,128)}, ...), condition=%wide.region_4.5_spmd.clone, body=%wide.region_3.4_spmd.clone.sunk | while | flops 100925440 | bytes 1837663 | solution.py:24
  326.2 1.4 fusion.142
  329.2 1.4 fusion.142
  332.2 1.4 fusion.142
  333.6 1.4 fusion.142
  336.6 1.4 fusion.142
  338.1 1.4 fusion.142
  341.1 1.4 fusion.142
  344.0 1.4 fusion.142
  348.5 1.4 fusion.142
  351.4 1.4 fusion.142
  354.4 1.4 fusion.142
  355.9 1.4 fusion.142
  358.9 1.4 fusion.142
  360.3 1.4 fusion.142
  370.7 44.7 %while.37 = (s32[]{:T(128)}, f32[4,128,128]{2,1,0:T(8,128)S(1)}, bf16[8,4,128,128]{3,2,0,1:T(8,128)(2,1)S(1)}, f32[8,4,128,128]{2,3,1,0:T(8,128)}, f32[8,4,128,1...) while((s32[]{:T(128)}, f32[4,128,128]{2,1,0:T(8,128)S(1)}, ...), condition=%wide.region_7.8_spmd, body=%wide.region_6.7_spmd.sunk | while | flops 402915328 | bytes 3804253 | solution.py:115
  416.2 20.2 %all_to_all.58 = bf16[1024,4,128]{2,1,0:T(4,128)(2,1)S(1)} all-to-all(bf16[1024,4,128]{2,1,0:T(4,128)(2,1)S(1)} %copy.30), channel_id=1, replica_groups=mesh['outer'=32,'inner'=8] {'inner'}, dimensions={0} | all-to-all | bytes 2097152 | tf_op jit(solution)/shard_map/all_to_all | solution.py:117
  436.6 1.6 copy.33
  (123 shorter events, 87.7 us)
Async XLA Ops:
  6.5 11.1 %all-to-all-start.1 = ((bf16[128,8,4]{0,2,1:T(4,128)(2,1)}), bf16[128,8,4]{0,2,1:T(4,128)(2,1)S(1)}, u32[]{:S(2)}, u32[]{:S(2)}) async-start(bf16[128,8,4]{0,2,1:T(4,128)(2,1)} %bitcast.145), calls=%async_computation.1 | async-start | bytes 16384 | tf_op jit(solution)/shard_map/all_to_all | solution.py:73
  13.0 8.8 %copy-start.3 = (bf16[128,32,128]{2,1,0:T(8,128)(2,1)S(1)}, bf16[128,32,128]{2,1,0:T(8,128)(2,1)}, u32[]{:S(2)}) copy-start(bf16[128,32,128]{2,1,0:T(8,128)(2,1)} %param.12) | copy-start | bytes 3145732
  17.6 19.3 %all-to-all-start = ((bf16[128,32,128]{2,0,1:T(8,128)(2,1)}), bf16[128,32,128]{2,0,1:T(8,128)(2,1)S(1)}, u32[]{:S(2)}, u32[]{:S(2)}) async-start(bf16[128,32,128]{2,0,1:T(8,128)(2,1)} %copy.24), calls=%async_computation | async-start | bytes 2097152 | tf_op jit(solution)/shard_map/all_to_all | solution.py:71
  36.9 40.5 %all-to-all-start.2 = ((bf16[128,32,128]{2,0,1:T(8,128)(2,1)}), bf16[128,32,128]{2,0,1:T(8,128)(2,1)S(1)}, u32[]{:S(2)}, u32[]{:S(2)}) async-start(bf16[128,32,128]{2,0,1:T(8,128)(2,1)} %copy.25), calls=%async_computation.2 | async-start | bytes 2097152 | tf_op jit(solution)/shard_map/all_to_all | solution.py:72
  41.3 184.0 %all-gather.5.cloned.1.call-start = ((), (), s32[]{:S(2)}) async-start(), calls=%async_computation.5 | async-start | bytes 8650752 | tf_op jit(solution)/shard_map/all_gather | solution.py:14
  72.6 1.3 copy-start
  77.4 2.2 copy-start.1
  77.4 3.0 copy-start.2
  124.1 1.6 copy-start.4
  125.0 198.2 %all-gather.7.cloned.1.call-start = ((), (), s32[]{:S(2)}) async-start(), calls=%async_computation.6 | async-start | bytes 8650752 | tf_op jit(solution)/shard_map/all_gather | solution.py:14
  127.2 20.2 %all-to-all-start.3 = ((bf16[128,32,128]{2,0,1:T(8,128)(2,1)}), bf16[128,32,128]{2,0,1:T(8,128)(2,1)S(1)}, u32[]{:S(2)}, u32[]{:S(2)}) async-start(bf16[128,32,128]{2,0,1:T(8,128)(2,1)} %copy.27), calls=%async_computation.3 | async-start | bytes 2097152 | tf_op jit(solution)/shard_map/all_to_all | solution.py:70
Sparse Core Ops, SparseCore 0:
  125.1 100.0 all-gather.4
  227.8 95.4 all-gather.6
where the time goes:
time: 451 us; the launch traced here: 445 us
  waiting for transfers between devices  198 us (44%)
  matrix products  160 us (35%)
  blocking collectives  20.2 us (4%)
  starting transfers between devices  20.1 us (4%)
  local copies, waits for them, and re-layouts  17.2 us (4%)
  between operations  13.9 us (3%)
  other arithmetic  13.7 us (3%)
    all_gather x2, waiting for transfers between devices, prefix(): everything = jax.tree.map(lambda part: lax.all_gather(part, axis), x)  167 us
    dot_general x32, matrix products, combine_pairs(): jnp.einsum('hij,hjk->hik', trans_b, offset_a, precision=HIGH) + offset_b  45.6 us
    all_to_all x1, blocking collectives, shards(): lax.all_to_all(token_major, 'inner', split_axis=0, concat_axis=1, tiled=T...  20.2 us
    dot_general x6, matrix products, unit_lower_inverse(): inverse = inverse + jnp.dot(inverse, power, precision=HIGH)  15.1 us
    all_to_all x1, waiting for transfers between devices, shards(): lax.all_to_all(query, 'inner', split_axis=1, concat_axis=0, tiled=True)  15 us
    all_to_all x1, waiting for transfers between devices, shards(): lax.all_to_all(keys, 'inner', split_axis=1, concat_axis=0, tiled=True)  13.5 us
    dot_general x8, matrix products, pair_step(): jnp.einsum('hcd,hce->hde', kpart, change, precision=HIGH)  13.3 us
    dot_general x8, matrix products, pair_step(): product = jnp.einsum('hcd,hde->hce', wpart, carried, precision=HIGH)  12.3 us
  transfers between devices with their start and end apart: 6, of which 5 were waited for; matrix products, arithmetic and copies ran while one was open for 11% of the time, Pallas kernels for 0%

commit v1 on v0

v1 whole, which is shorter than its diff:
```python
import functools

import jax
import jax.numpy as jnp
from jax import lax
from jax.experimental import pallas as pl
from jax.experimental.pallas import tpu as pltpu
from jax.sharding import Mesh
from jax.sharding import PartitionSpec as P

SPAN = 128
DIM = 128
SUPER = 4
STEPS = 8
PACK = 136
F32 = jnp.float32
BF16 = jnp.bfloat16
EPS = 1e-06
GROUP = ("x", "y", "core")
EVERY = ("z", "x", "y", "core")


def split(x):
    high = x.astype(BF16)
    low = (x - high.astype(F32)).astype(BF16)
    return high, low


def lanes(parts):
    return jnp.concatenate(parts, axis=1)


def rows(parts):
    return jnp.concatenate(parts, axis=0)


def mm(a, b):
    return jnp.dot(a, b, preferred_element_type=F32)


def mm_nt(a, b):
    return lax.dot_general(a, b, (((1,), (1,)), ((), ())), preferred_element_type=F32)


def mm_tn(a, b):
    return lax.dot_general(a, b, (((0,), (0,)), ((), ())), preferred_element_type=F32)


def mm_cat(a_cat, b):
    high, low = split(b)
    depth = b.shape[0]
    return mm(a_cat, rows([high, high])) + mm(a_cat[:, :depth], low)


def cat(x):
    return lanes(split(x))


def mm3(a, b):
    return mm_cat(cat(a), b)


def inv_sqrt(x):
    x = x + EPS
    guess = lax.rsqrt(x)
    return guess * (1.5 - 0.5 * x * guess * guess)


def index_grids():
    row = lax.broadcasted_iota(jnp.int32, (SPAN, SPAN), 0)
    col = lax.broadcasted_iota(jnp.int32, (SPAN, SPAN), 1)
    return row, col


def keys_kernel(kp_ref, xu_ref, w_ref, t_ref, p_ref, pcum_ref, pup_ref, carry):
    step = pl.program_id(0)
    row, col = index_grids()
    diag = row == col
    eye = jnp.where(diag, 1.0, 0.0).astype(F32)
    n = range(SUPER)

    @pl.when(step == 0)
    def _():
        for i in n:
            carry[i] = eye

    k = [kp_ref[i, 0, :SPAN, :] for i in n]
    b_row = [kp_ref[i, 0, SPAN : SPAN + 1, :].astype(F32) for i in n]
    gram = [mm_nt(k[i], k[i]) for i in n]
    on_diag = [jnp.where(diag, gram[i], 0.0) for i in n]
    r_row = [inv_sqrt(jnp.sum(on_diag[i], axis=0, keepdims=True)) for i in n]
    r_col = [inv_sqrt(jnp.sum(on_diag[i], axis=1, keepdims=True)) for i in n]
    b_col = [jnp.sum(jnp.where(diag, b_row[i], 0.0), axis=1, keepdims=True) for i in n]
    strict = [
        jnp.where(row > col, gram[i] * (b_col[i] * r_col[i]) * r_row[i], 0.0) for i in n
    ]
    x = [eye - jnp.where((row >> 1) == (col >> 1), strict[i], 0.0) for i in n]
    for level in range(1, 7):
        below = ((row >> level) ^ (col >> level)) == 1
        x_cat = [cat(x[i]) for i in n]
        part = [mm_cat(x_cat[i], jnp.where(below, strict[i], 0.0)) for i in n]
        x = [x[i] - mm3(part[i], x[i]) for i in n]
    xu = [x[i] * r_col[i] * b_row[i] for i in n]
    for i in n:
        xu_ref[i, 0] = cat(xu[i])
    w = [mm(cat(xu[i] * r_row[i]), rows([k[i], k[i]])) for i in n]
    w_split = [split(w[i]) for i in n]
    for i in n:
        w_ref[i, 0] = lanes(w_split[i])
    t = [eye - mm_tn(rows([k[i], k[i]]), rows(w_split[i])) for i in n]
    t_cat = [cat(t[i]) for i in n]
    for i in n:
        t_ref[i, 0] = t_cat[i]
    before = [carry[i] for i in n]
    for i in n:
        p_ref[i, 0] = cat(before[i])
    after = [mm_cat(t_cat[i], before[i]) for i in n]
    for i in n:
        carry[i] = after[i]

    @pl.when(step == STEPS - 1)
    def _():
        one = mm3(carry[1], carry[0])
        two = mm3(carry[3], carry[2])
        pcum_ref[0] = eye
        pcum_ref[1] = carry[0]
        pcum_ref[2] = one
        pcum_ref[3] = mm3(carry[2], one)
        pcum_ref[4] = mm3(two, one)
        pup_ref[0] = carry[1]
        pup_ref[1] = carry[2]
        pup_ref[2] = carry[3]
        pup_ref[3] = two


def values_kernel(kp_ref, v_ref, xu_ref, t_ref, pup_ref, u_ref, o_ref, ocum_ref, carry):
    step = pl.program_id(0)
    n = range(SUPER)

    @pl.when(step == 0)
    def _():
        carry[...] = jnp.zeros_like(carry)

    k = [kp_ref[i, 0, :SPAN, :] for i in n]
    v = [v_ref[i, 0] for i in n]
    u = [mm(xu_ref[i, 0], rows([v[i], v[i]])) for i in n]
    for i in n:
        u_ref[i, 0] = u[i]
    before = [carry[i] for i in n]
    for i in n:
        o_ref[i, 0] = before[i]
    own = [mm_tn(rows([k[i], k[i]]), rows(split(u[i]))) for i in n]
    for i in n:
        carry[i] = mm_cat(t_ref[i, 0], before[i]) + own[i]

    @pl.when(step == STEPS - 1)
    def _():
        one = mm3(pup_ref[0], carry[0]) + carry[1]
        two = mm3(pup_ref[2], carry[2]) + carry[3]
        ocum_ref[0] = jnp.zeros_like(one)
        ocum_ref[1] = carry[0]
        ocum_ref[2] = one
        ocum_ref[3] = mm3(pup_ref[1], one) + carry[2]
        ocum_ref[4] = mm3(pup_ref[3], one) + two


def pair_trans_kernel(up_ref, own_ref, other_ref, tup_ref, et_ref, total_ref):
    up = up_ref[0] != 0
    row, col = index_grids()
    eye = jnp.where(row == col, 1.0, 0.0).astype(F32)
    own, other = own_ref[...], other_ref[...]
    upper = jnp.where(up, own, other)
    lower = jnp.where(up, other, own)
    tup_ref[...] = upper
    et_ref[...] = jnp.where(up, other, eye)
    total_ref[...] = mm3(upper, lower)


def quad_trans_kernel(up_ref, own_ref, other_ref, et_ref, tup_ref, et_out_ref):
    up = up_ref[0] != 0
    own, other, et = own_ref[...], other_ref[...], et_ref[...]
    tup_ref[...] = jnp.where(up, own, other)
    et_out_ref[...] = jnp.where(up, mm3(et, other), et)


def pair_offset_kernel(up_ref, own_ref, other_ref, tup_ref, total_ref, eo_ref):
    up = up_ref[0] != 0
    own, other = own_ref[...], other_ref[...]
    lower = jnp.where(up, other, own)
    upper = jnp.where(up, own, other)
    total_ref[...] = mm3(tup_ref[...], lower) + upper
    eo_ref[...] = jnp.where(up, other, 0.0)


def quad_offset_kernel(up_ref, own_ref, other_ref, tup_ref, et_ref, eo_ref, total_ref, eo_out_ref):
    up = up_ref[0] != 0
    own, other, eo = own_ref[...], other_ref[...], eo_ref[...]
    lower = jnp.where(up, other, own)
    upper = jnp.where(up, own, other)
    total_ref[...] = mm3(tup_ref[...], lower) + upper
    eo_out_ref[...] = jnp.where(up, mm3(et_ref[...], other) + eo, eo)


def output_kernel(
    up_ref, other_ref, et_ref, eo_ref, pcum_ref, ocum_ref,
    q_ref, kp_ref, w_ref, u_ref, p_ref, o_ref, out_ref, start,
):
    step = pl.program_id(0)
    n = range(SUPER)

    @pl.when(step == 0)
    def _():
        eo = eo_ref[...]
        first = jnp.where(up_ref[0] != 0, mm3(et_ref[...], other_ref[...]) + eo, eo)
        for i in n:
            start[i] = mm3(pcum_ref[i], first) + ocum_ref[i]

    row, col = index_grids()
    q = [q_ref[i, 0] for i in n]
    k = [kp_ref[i, 0, :SPAN, :] for i in n]
    scale = [
        inv_sqrt(jnp.sum(jnp.square(q[i].astype(F32)), axis=1, keepdims=True)) for i in n
    ]
    scores = [split(jnp.where(row >= col, mm_nt(q[i], k[i]), 0.0)) for i in n]
    state = [mm_cat(p_ref[i, 0], start[i]) + o_ref[i, 0] for i in n]
    delta = [u_ref[i, 0] - mm_cat(w_ref[i, 0], state[i]) for i in n]
    s_split = [split(state[i]) for i in n]
    d_split = [split(delta[i]) for i in n]
    for i in n:
        left = lanes([q[i], scores[i][0]])
        total = (
            mm(left, rows([s_split[i][0], d_split[i][0]]))
            + mm(left, rows([s_split[i][1], d_split[i][1]]))
            + mm(scores[i][1], d_split[i][0])
        )
        out_ref[i, 0] = (total * scale[i]).astype(BF16)


def block(*tail):
    return pl.BlockSpec((SUPER, 1) + tail, lambda b: (0, b, 0, 0))


def whole(*shape):
    return pl.BlockSpec(shape, lambda b: (0,) * len(shape))


def like(*shape, dtype=F32):
    return jax.ShapeDtypeStruct(shape, dtype)


def cost(passes, nbytes):
    return pl.CostEstimate(
        flops=2 * SUPER * STEPS * passes * SPAN**3, bytes_accessed=nbytes, transcendentals=0
    )


SMEM = pl.BlockSpec(memory_space=pltpu.SMEM)
VMEM = pl.BlockSpec(memory_space=pltpu.VMEM)
PARAMS = pltpu.CompilerParams(vmem_limit_bytes=48 * 1024 * 1024)
MIB = 1 << 20


def small(kernel, outs, *args):
    return pl.pallas_call(
        kernel,
        out_shape=[like(DIM, DIM)] * outs,
        in_specs=[SMEM] + [VMEM] * (len(args) - 1),
        out_specs=[VMEM] * outs,
        cost_estimate=pl.CostEstimate(
            flops=12 * DIM**3, bytes_accessed=65536 * len(args), transcendentals=0
        ),
    )(*args)


def exchange(x, distance, size):
    return lax.ppermute(x, "z", [(i, i ^ distance) for i in range(size)])


def shards(query, keys, value, beta):
    depth = lax.axis_size("z")
    z = lax.axis_index("z")
    up1, up2, up4 = [((z >> s) & 1).astype(jnp.int32)[None] for s in (0, 1, 2)]

    def heads_first(array):
        return jnp.transpose(array, (1, 0, 2))

    def to_heads(array):
        return lax.all_to_all(array, GROUP, split_axis=0, concat_axis=0, tiled=True)

    def by_super(array):
        return array.reshape((SUPER, STEPS) + array.shape[1:])

    gates = jnp.pad(beta.T[:, None, :], ((0, 0), (0, PACK - SPAN - 1), (0, 0)))
    packed = jnp.concatenate([heads_first(keys), gates], axis=1)
    vt, qt = heads_first(value), heads_first(query)
    kp = to_heads(packed)
    vt, kp = lax.optimization_barrier((vt, kp))
    vh = to_heads(vt)
    qt, vh = lax.optimization_barrier((qt, vh))
    qh = to_heads(qt)
    kp, vh, qh = by_super(kp), by_super(vh), by_super(qh)

    full = (SUPER, STEPS)
    xu, w, t, p, pcum, pup = pl.pallas_call(
        keys_kernel,
        grid=(STEPS,),
        in_specs=[block(PACK, DIM)],
        out_specs=[block(SPAN, 2 * SPAN)] * 4 + [whole(5, DIM, DIM), whole(4, DIM, DIM)],
        out_shape=[like(*full, SPAN, 2 * SPAN, dtype=BF16)] * 4
        + [like(5, DIM, DIM), like(4, DIM, DIM)],
        scratch_shapes=[pltpu.VMEM((SUPER, DIM, DIM), F32)],
        compiler_params=PARAMS,
        cost_estimate=cost(44, 9 * MIB),
        name="keys_terms",
    )(kp)

    trans = pcum[4]
    tup1, et1, trans2 = small(pair_trans_kernel, 3, up1, trans, exchange(trans, 1, depth))
    tup2, et2 = small(quad_trans_kernel, 2, up2, trans2, exchange(trans2, 2, depth), et1)

    u, o, ocum = pl.pallas_call(
        values_kernel,
        grid=(STEPS,),
        in_specs=[
            block(PACK, DIM), block(SPAN, DIM), block(SPAN, 2 * SPAN), block(SPAN, 2 * SPAN),
            whole(4, DIM, DIM),
        ],
        out_specs=[block(SPAN, DIM)] * 2 + [whole(5, DIM, DIM)],
        out_shape=[like(*full, SPAN, DIM)] * 2 + [like(5, DIM, DIM)],
        scratch_shapes=[pltpu.VMEM((SUPER, DIM, DIM), F32)],
        compiler_params=PARAMS,
        cost_estimate=cost(7, 10 * MIB),
        name="values_terms",
    )(kp, vh, xu, t, pup)

    offset = ocum[4]
    off2, eo1 = small(pair_offset_kernel, 2, up1, offset, exchange(offset, 1, depth), tup1)
    off4, eo2 = small(
        quad_offset_kernel, 2, up2, off2, exchange(off2, 2, depth), tup2, et1, eo1
    )
    other = exchange(off4, 4, depth)

    out = pl.pallas_call(
        output_kernel,
        grid=(STEPS,),
        in_specs=[
            SMEM, whole(DIM, DIM), whole(DIM, DIM), whole(DIM, DIM),
            whole(5, DIM, DIM), whole(5, DIM, DIM),
            block(SPAN, DIM), block(PACK, DIM), block(SPAN, 2 * SPAN), block(SPAN, DIM),
            block(SPAN, 2 * SPAN), block(SPAN, DIM),
        ],
        out_specs=block(SPAN, DIM),
        out_shape=like(*full, SPAN, DIM, dtype=BF16),
        scratch_shapes=[pltpu.VMEM((SUPER, DIM, DIM), F32)],
        compiler_params=PARAMS,
        cost_estimate=cost(12, 11 * MIB),
        name="mix_output",
    )(up4, other, et2, eo2, pcum, ocum, qh, kp, w, u, p, o)
    back = to_heads(out.reshape(SUPER * STEPS, SPAN, DIM))
    return jnp.transpose(back, (1, 0, 2))


def solution(mesh):
    fine = Mesh(mesh.devices.reshape(8, 4, 4, 2), EVERY)
    placed = (P(EVERY, None, None), P(EVERY, None, None), P(EVERY, None, None), P(EVERY, None))
    return jax.shard_map(
        shards,
        mesh=fine,
        in_specs=placed,
        out_specs=P(EVERY, None, None),
        check_vma=False,
    )
```

time: 451 us -> 159 us (0.35); the launches traced: 445 us -> 158 us
  waiting for transfers between devices: 198 us -> 34.1 us
  matrix products: 160 us -> 0 us
  Pallas kernels: 0 us -> 49.7 us
  between operations: 13.9 us -> 0.1 us
  other arithmetic: 13.7 us -> 1.1 us
  starting transfers between devices: 20.1 us -> 28.1 us
  blocking collectives: 20.2 us -> 27.3 us
    all_gather x2 -> x0, waiting for transfers between devices: 167 us -> none  [prefix(): everything = jax.tree.map(lambda part: lax.all_gather(part, axis), x)]
    dot_general x95 -> x0, matrix products: 160 us -> none  [the longest x32 45.6 us: combine_pairs(): jnp.einsum('hij,hjk->hik', trans_b, offset_a, precision=HIGH) + offset_b]
    pallas_call x0 -> x7, Pallas kernels: none -> 49.7 us  [the longest x1 25.2 us: shards(): pl.pallas_call(keys_kernel, grid=(STEPS,), in_specs=[block(PACK, DIM)], o...]
    ppermute x0 -> x5, starting transfers between devices: none -> 11.7 us  [exchange(): return lax.ppermute(x, 'z', [(i, i ^ distance) for i in range(size)])]
    neg x8 -> x0, other arithmetic: 8.13 us -> none  [pair_step(): -product[..., :width]]
    unnamed x13 -> x34, local copies, waits for them, and re-layouts: 7.54 us -> 15.4 us
    all_to_all x1, blocking collectives: 20.2 us -> 27.3 us  [to_heads(): return lax.all_to_all(array, GROUP, split_axis=0, concat_axis=0, tiled=True)]
    all_to_all x4 -> x3, starting transfers between devices: 20.1 us -> 16.5 us  [to_heads(): return lax.all_to_all(array, GROUP, split_axis=0, concat_axis=0, tiled=True)]
  transfers between devices with their start and end apart: 6 -> 8, of which waited for: 5 -> 4; matrix products, arithmetic and copies ran while one was open for 11% -> 2% of each run, Pallas kernels for 0% -> 26%
where the time goes in v1:
time: 159 us; the launch traced here: 158 us
  Pallas kernels  49.7 us (31%)
  waiting for transfers between devices  34.1 us (21%)
  starting transfers between devices  28.1 us (18%)
  blocking collectives  27.3 us (17%)
  local copies, waits for them, and re-layouts  17.7 us (11%)
    all_to_all x3, waiting for transfers between devices, to_heads(): return lax.all_to_all(array, GROUP, split_axis=0, concat_axis=0, tiled=True)  31.8 us
    all_to_all x1, blocking collectives, to_heads(): return lax.all_to_all(array, GROUP, split_axis=0, concat_axis=0, tiled=True)  27.3 us
    pallas_call x1, Pallas kernels, shards(): pl.pallas_call(keys_kernel, grid=(STEPS,), in_specs=[block(PACK, DIM)], o...  25.2 us
    all_to_all x3, starting transfers between devices, to_heads(): return lax.all_to_all(array, GROUP, split_axis=0, concat_axis=0, tiled=True)  16.5 us
    unnamed x34, local copies, waits for them, and re-layouts  15.4 us
    ppermute x5, starting transfers between devices, exchange(): return lax.ppermute(x, 'z', [(i, i ^ distance) for i in range(size)])  11.7 us
    pallas_call x1, Pallas kernels, shards(): pl.pallas_call(output_kernel, grid=(STEPS,), in_specs=[SMEM, whole(DIM, D...  9.31 us
    pallas_call x1, Pallas kernels, shards(): pl.pallas_call(values_kernel, grid=(STEPS,), in_specs=[block(PACK, DIM),...  8.34 us
  transfers between devices with their start and end apart: 8, of which 4 were waited for; matrix products, arithmetic and copies ran while one was open for 2% of the time, Pallas kernels for 26%

profile of v1, /device:TPU:1, one launch (start us, length us, event | category | flops | bytes accessed | tf_op | source)
XLA Modules:
  0.0 158.1 jit_solution(17630626909600568283)
XLA Ops:
  0.0 0.0 copy-start.14
  0.0 1.6 %copy.23 = bf16[128,32,128]{2,0,1:T(8,128)(2,1)S(1)} copy(bf16[128,32,128]{2,1,0:T(8,128)(2,1)} %param.5) | data formatting | bytes 2097152 | tf_op args[1]
  1.6 0.0 copy-done.14
  1.7 0.0 copy-start.8
  1.7 1.1 fusion.1
  2.8 8.6 %all-to-all-start = ((bf16[32,136,128]{2,1,0:T(8,128)(2,1)}), bf16[32,136,128]{2,1,0:T(8,128)(2,1)S(1)}, u32[]{:S(2)}, u32[]{:S(2)}) async-start(bf16[32,136,128]{2,1,0:T(8,128)(2,1)} %fusion.1), calls=%async_computation | async-start | bytes 2228224 | tf_op jit(solution)/shard_map/all_to_all | solution.py:288
  11.4 0.0 copy-done.8
  11.4 1.4 copy.24
  12.8 0.0 copy-start.9
  12.8 16.3 %all-to-all-done = bf16[32,136,128]{2,1,0:T(8,128)(2,1)S(1)} async-done(((bf16[32,136,128]{2,1,0:T(8,128)(2,1)}), bf16[32,136,128]{2,1,0:T(8,128)(2,1)S(1)}, u32[]{:S(2)}, u32[]{:S(2)}) %all-to-all-start) | async-done | bytes 1114144 | tf_op jit(solution)/shard_map/all_to_all | solution.py:288
  29.0 3.9 %all-to-all-start.1 = ((bf16[32,128,128]{2,1,0:T(8,128)(2,1)}), bf16[32,128,128]{2,1,0:T(8,128)(2,1)S(1)}, u32[]{:S(2)}, u32[]{:S(2)}) async-start(bf16[32,128,128]{2,1,0:T(8,128)(2,1)} %bitcast.23), calls=%async_computation.1 | async-start | bytes 2097152 | tf_op jit(solution)/shard_map/all_to_all | solution.py:288
  33.0 0.0 copy-done.9
  33.0 1.4 copy.22
  34.4 15.5 %all-to-all-done.1 = bf16[32,128,128]{2,1,0:T(8,128)(2,1)S(1)} async-done(((bf16[32,128,128]{2,1,0:T(8,128)(2,1)}), bf16[32,128,128]{2,1,0:T(8,128)(2,1)S(1)}, u32[]{:S(2)}, u32[]{:S(2)}) %all-to-all-start.1) | async-done | bytes 1048608 | tf_op jit(solution)/shard_map/all_to_all | solution.py:288
  49.9 4.0 %all-to-all-start.2 = ((bf16[32,128,128]{2,1,0:T(8,128)(2,1)}), bf16[32,128,128]{2,1,0:T(8,128)(2,1)S(1)}, u32[]{:S(2)}, u32[]{:S(2)}) async-start(bf16[32,128,128]{2,1,0:T(8,128)(2,1)} %bitcast.30), calls=%async_computation.2 | async-start | bytes 2097152 | tf_op jit(solution)/shard_map/all_to_all | solution.py:288
  53.8 25.2 %keys_terms.1 = (bf16[4,8,128,256]{3,2,1,0:T(8,128)(2,1)S(1)}, bf16[4,8,128,256]{3,2,1,0:T(8,128)(2,1)S(1)}, bf16[4,8,128,256]{3,2,1,0:T(8,128)(2,1)}, bf16[4,8,...) custom-call(bf16[4,8,136,128]{3,2,1,0:T(8,128)(2,1)S(1)} %bitcast.24), custom_call_target="tpu_custom_call" | custom-call | flops 5905580032 | bytes 9437184 | tf_op jit(solution)/shard_map/keys_terms/pallas_call | solution.py:304
  79.0 0.0 copy-start
  79.0 1.4 copy-done
  80.4 0.0 copy-start.3
  80.4 1.4 copy-done.3
  81.8 0.6 slice_bitcast_fusion.own_ref
  82.4 1.6 %collective-permute-start.1 = (f32[128,128]{1,0:T(8,128)}, f32[128,128]{1,0:T(8,128)}, u32[]{:S(2)}, u32[]{:S(2)}) collective-permute-start(f32[128,128]{1,0:T(8,128)} %slice_bitcast_fusion.own_ref), channel_id=1, source_target_pairs={{0,32},{32,0},{64,96},{96,64},{128,160},{160,128},{192,224},{224,1... | collective-permute-start | bytes 196616 | tf_op jit(solution)/shard_map/ppermute | solution.py:276
  84.0 8.3 %values_terms.1 = (f32[4,8,128,128]{3,2,1,0:T(8,128)S(1)}, f32[4,8,128,128]{3,2,1,0:T(8,128)}, f32[5,128,128]{2,1,0:T(8,128)S(1)}) custom-call(bf16[4,8,136,128]{3,2,1,0:T(8,128)(2,1)S(1)} %bitcast.25, bf16[4,8,128,128]{3,2,1,0:T(8,128)(2,1)S(1)} %bitcast.28, bf16[4,8,128,256]{3,2,1,0:T(8,128)(2,1)} %copy-done.3, ...), custom_call_target="tpu_custom_call" | custom-call | flops 939524096 | bytes 10485760 | tf_op jit(solution)/shard_map/values_terms/pallas_call | solution.py:321
  92.4 0.0 copy-start.2
  92.4 1.4 copy-done.2
  93.8 0.0 copy-start.4
  93.8 0.7 copy-done.4
  94.5 0.0 copy-start.10
  94.5 0.0 collective-permute-start
  94.5 0.0 collective-permute-done.1.other_ref
  94.5 1.7 %shard_map.46 = (f32[128,128]{1,0:T(8,128)}, f32[128,128]{1,0:T(8,128)}, f32[128,128]{1,0:T(8,128)}) custom-call(s32[1]{0:T(128)} %bitcast.2.up_ref, f32[128,128]{1,0:T(8,128)} %slice_bitcast_fusion.own_ref, f32[128,128]{1,0:T(8,128)} %collective-permute-done.1.other_ref), custom_call_target="tpu_custom_call" | custom-call | flops 25165824 | bytes 196608 | tf_op jit(solution)/shard_map/pallas_call | solution.py:264
  96.2 3.0 %collective-permute-start.3 = (f32[128,128]{1,0:T(8,128)}, f32[128,128]{1,0:T(8,128)S(1)}, u32[]{:S(2)}, u32[]{:S(2)}) collective-permute-start(f32[128,128]{1,0:T(8,128)} %get-tuple-element.37.own_ref), channel_id=1, source_target_pairs={{0,64},{32,96},{64,0},{96,32},{128,192},{160,224},{192,128},{224,1... | collective-permute-start | bytes 196616 | tf_op jit(solution)/shard_map/ppermute | solution.py:276
  99.2 0.0 collective-permute-done.other_ref
  99.2 0.0 copy-start.11
  99.2 0.0 copy-done.10
  99.2 0.6 copy-done.11
  99.8 1.7 %shard_map.47 = (f32[128,128]{1,0:T(8,128)}, f32[128,128]{1,0:T(8,128)}) custom-call(s32[1]{0:T(128)} %bitcast.2.up_ref, f32[128,128]{1,0:T(8,128)} %copy-done.10, f32[128,128]{1,0:T(8,128)} %copy-done.11, f32[128,128]{1,0:T(8,128)} %get-tuple-element.35.tup_ref), custom_call_target="tpu_custom_call" | custom-call | flops 25165824 | bytes 262144 | tf_op jit(solution)/shard_map/pallas_call | solution.py:264
  101.5 1.4 collective-permute-start.2
  102.9 0.0 collective-permute-done.3.other_ref
  102.9 0.0 copy-start.12
  102.9 0.6 copy-done.12
  103.5 1.7 %shard_map.48 = (f32[128,128]{1,0:T(8,128)}, f32[128,128]{1,0:T(8,128)}) custom-call(s32[1]{0:T(128)} %bitcast.1.up_ref, f32[128,128]{1,0:T(8,128)} %get-tuple-element.37.own_ref, f32[128,128]{1,0:T(8,128)} %copy-done.12, f32[128,128]{1,0:T(8,128)} %get-tuple-element.38.et_ref), custom_call_target="tpu_custom_call" | custom-call | flops 25165824 | bytes 262144 | tf_op jit(solution)/shard_map/pallas_call | solution.py:264
  105.2 0.5 collective-permute-done.2.other_ref
  105.7 0.0 copy-start.13
  105.7 0.6 copy-done.13
  106.3 1.8 %shard_map.49 = (f32[128,128]{1,0:T(8,128)}, f32[128,128]{1,0:T(8,128)}) custom-call(s32[1]{0:T(128)} %bitcast.1.up_ref, f32[128,128]{1,0:T(8,128)} %get-tuple-element.36.own_ref, f32[128,128]{1,0:T(8,128)} %copy-done.13, f32[128,128]{1,0:T(8,128)} %get-tuple-element.39.tup_ref, f32[128,128]{1,0:T(8,128)} %get-tuple-element.38.et_ref, ...), custom_call_target="tpu_custom_call" | custom-call | flops 25165824 | bytes 393216 | tf_op jit(solution)/shard_map/pallas_call | solution.py:264
  108.2 5.6 %collective-permute-start.4 = (f32[128,128]{1,0:T(8,128)}, f32[128,128]{1,0:T(8,128)S(1)}, u32[]{:S(2)}, u32[]{:S(2)}) collective-permute-start(f32[128,128]{1,0:T(8,128)} %get-tuple-element.41), channel_id=1, source_target_pairs={{0,128},{32,160},{64,192},{96,224},{128,0},{160,32},{192,64},{224,... | collective-permute-start | bytes 196616 | tf_op jit(solution)/shard_map/ppermute | solution.py:276
  113.8 1.9 %collective-permute-done.4.other_ref = f32[128,128]{1,0:T(8,128)S(1)} collective-permute-done((f32[128,128]{1,0:T(8,128)}, f32[128,128]{1,0:T(8,128)S(1)}, u32[]{:S(2)}, u32[]{:S(2)}) %collective-permute-start.4) | collective-permute-done | bytes 65568 | tf_op jit(solution)/shard_map/ppermute | solution.py:276
  115.6 0.0 all-to-all-done.2
  115.6 0.0 copy-start.1
  115.6 1.6 %copy-done.1 = bf16[4,8,128,256]{3,2,1,0:T(8,128)(2,1)S(1)} copy-done((bf16[4,8,128,256]{3,2,1,0:T(8,128)(2,1)S(1)}, bf16[4,8,128,256]{3,2,1,0:T(8,128)(2,1)}, u32[]{:S(2)}) %copy-start.1) | copy-done | bytes 2097176
  117.2 0.0 copy-start.5
  117.2 1.0 copy-done.5
  118.2 0.0 copy-start.6
  118.2 0.8 copy-done.6
  119.0 0.0 copy-start.7
  119.0 0.8 copy-done.7
  119.9 9.3 %mix_output.1 = bf16[4,8,128,128]{3,2,1,0:T(8,128)(2,1)S(1)} custom-call(s32[1]{0:T(128)} %bitcast.up_ref, f32[128,128]{1,0:T(8,128)S(1)} %collective-permute-done.4.other_ref, f32[128,128]{1,0:T(8,128)S(1)} %copy-done.6, f32[128,128]{1,0:T(8,128)S(1)} %copy-done.7, f32[5,128,128]{2,1,0:T(8,128)S(1)} %get-tuple-element.34.pcum_ref, ...), custom_call_target="tpu_custom_call" | custom-call | flops 1610612736 | bytes 11534336 | tf_op jit(solution)/shard_map/mix_output/pallas_call | solution.py:343
  129.2 27.3 %all_to_all.20 = bf16[32,128,128]{2,1,0:T(8,128)(2,1)S(1)} all-to-all(bf16[32,128,128]{2,1,0:T(8,128)(2,1)S(1)} %bitcast.29), channel_id=1, replica_groups=mesh['z'=8,'x'=4,'y'=4,'core'=2] {'x','y','core'}, dimensions={0} | all-to-all | bytes 2097152 | tf_op jit(solution)/shard_map/all_to_all | solution.py:288
  156.5 1.6 %copy.17 = bf16[128,32,128]{2,1,0:T(8,128)(2,1)} copy(bf16[128,32,128]{2,0,1:T(8,128)(2,1)S(1)} %bitcast.32) | data formatting | bytes 2097152 | tf_op jit(solution)/shard_map/transpose | solution.py:360
  (2 shorter events, 0.0 us)
Async XLA Ops:
  0.0 1.7 %copy-start.14 = (bf16[128,32]{0,1:T(8,128)(2,1)S(1)}, bf16[128,32]{0,1:T(8,128)(2,1)}, u32[]{:S(2)}) copy-start(bf16[128,32]{0,1:T(8,128)(2,1)} %param.7) | copy-start | bytes 24580
  1.7 9.7 %copy-start.8 = (bf16[128,32,128]{2,1,0:T(8,128)(2,1)S(1)}, bf16[128,32,128]{2,1,0:T(8,128)(2,1)}, u32[]{:S(2)}) copy-start(bf16[128,32,128]{2,1,0:T(8,128)(2,1)} %param.6) | copy-start | bytes 3145732
  2.8 26.2 %all-to-all-start = ((bf16[32,136,128]{2,1,0:T(8,128)(2,1)}), bf16[32,136,128]{2,1,0:T(8,128)(2,1)S(1)}, u32[]{:S(2)}, u32[]{:S(2)}) async-start(bf16[32,136,128]{2,1,0:T(8,128)(2,1)} %fusion.1), calls=%async_computation | async-start | bytes 2228224 | tf_op jit(solution)/shard_map/all_to_all | solution.py:288
  12.8 20.2 %copy-start.9 = (bf16[128,32,128]{2,1,0:T(8,128)(2,1)S(1)}, bf16[128,32,128]{2,1,0:T(8,128)(2,1)}, u32[]{:S(2)}) copy-start(bf16[128,32,128]{2,1,0:T(8,128)(2,1)} %param.4) | copy-start | bytes 3145732
  29.0 20.8 %all-to-all-start.1 = ((bf16[32,128,128]{2,1,0:T(8,128)(2,1)}), bf16[32,128,128]{2,1,0:T(8,128)(2,1)S(1)}, u32[]{:S(2)}, u32[]{:S(2)}) async-start(bf16[32,128,128]{2,1,0:T(8,128)(2,1)} %bitcast.23), calls=%async_computation.1 | async-start | bytes 2097152 | tf_op jit(solution)/shard_map/all_to_all | solution.py:288
  49.9 65.7 %all-to-all-start.2 = ((bf16[32,128,128]{2,1,0:T(8,128)(2,1)}), bf16[32,128,128]{2,1,0:T(8,128)(2,1)S(1)}, u32[]{:S(2)}, u32[]{:S(2)}) async-start(bf16[32,128,128]{2,1,0:T(8,128)(2,1)} %bitcast.30), calls=%async_computation.2 | async-start | bytes 2097152 | tf_op jit(solution)/shard_map/all_to_all | solution.py:288
  79.0 1.4 copy-start
  80.4 1.4 copy-start.3
  82.4 12.1 %collective-permute-start.1 = (f32[128,128]{1,0:T(8,128)}, f32[128,128]{1,0:T(8,128)}, u32[]{:S(2)}, u32[]{:S(2)}) collective-permute-start(f32[128,128]{1,0:T(8,128)} %slice_bitcast_fusion.own_ref), channel_id=1, source_target_pairs={{0,32},{32,0},{64,96},{96,64},{128,160},{160,128},{192,224},{224,1... | collective-permute-start | bytes 196616 | tf_op jit(solution)/shard_map/ppermute | solution.py:276
  92.4 1.4 copy-start.2
  93.8 0.7 copy-start.4
  94.5 4.7 %copy-start.10 = (f32[128,128]{1,0:T(8,128)}, f32[128,128]{1,0:T(8,128)S(1)}, u32[]{:S(2)}) copy-start(f32[128,128]{1,0:T(8,128)S(1)} %slice_bitcast_fusion.1.own_ref) | copy-start | bytes 196612
  94.5 4.7 %collective-permute-start = (f32[128,128]{1,0:T(8,128)S(1)}, f32[128,128]{1,0:T(8,128)S(1)}, u32[]{:S(2)}, u32[]{:S(2)}) collective-permute-start(f32[128,128]{1,0:T(8,128)S(1)} %slice_bitcast_fusion.1.own_ref), channel_id=1, source_target_pairs={{0,32},{32,0},{64,96},{96,64},{128,160},{160,128},{192,224},{224,1... | collective-permute-start | bytes 196616 | tf_op jit(solution)/shard_map/ppermute | solution.py:276
  96.2 6.7 %collective-permute-start.3 = (f32[128,128]{1,0:T(8,128)}, f32[128,128]{1,0:T(8,128)S(1)}, u32[]{:S(2)}, u32[]{:S(2)}) collective-permute-start(f32[128,128]{1,0:T(8,128)} %get-tuple-element.37.own_ref), channel_id=1, source_target_pairs={{0,64},{32,96},{64,0},{96,32},{128,192},{160,224},{192,128},{224,1... | collective-permute-start | bytes 196616 | tf_op jit(solution)/shard_map/ppermute | solution.py:276
  99.2 0.6 copy-start.11
  101.5 4.2 %collective-permute-start.2 = (f32[128,128]{1,0:T(8,128)}, f32[128,128]{1,0:T(8,128)S(1)}, u32[]{:S(2)}, u32[]{:S(2)}) collective-permute-start(f32[128,128]{1,0:T(8,128)} %get-tuple-element.36.own_ref), channel_id=1, source_target_pairs={{0,64},{32,96},{64,0},{96,32},{128,192},{160,224},{192,128},{224,1... | collective-permute-start | bytes 196616 | tf_op jit(solution)/shard_map/ppermute | solution.py:276
  102.9 0.6 copy-start.12
  105.7 0.6 copy-start.13
  108.2 7.5 %collective-permute-start.4 = (f32[128,128]{1,0:T(8,128)}, f32[128,128]{1,0:T(8,128)S(1)}, u32[]{:S(2)}, u32[]{:S(2)}) collective-permute-start(f32[128,128]{1,0:T(8,128)} %get-tuple-element.41), channel_id=1, source_target_pairs={{0,128},{32,160},{64,192},{96,224},{128,0},{160,32},{192,64},{224,... | collective-permute-start | bytes 196616 | tf_op jit(solution)/shard_map/ppermute | solution.py:276
  115.6 1.6 %copy-start.1 = (bf16[4,8,128,256]{3,2,1,0:T(8,128)(2,1)S(1)}, bf16[4,8,128,256]{3,2,1,0:T(8,128)(2,1)}, u32[]{:S(2)}) copy-start(bf16[4,8,128,256]{3,2,1,0:T(8,128)(2,1)} %copy-done) | copy-start | bytes 6291460
  117.2 1.0 copy-start.5
  118.2 0.8 copy-start.6
  119.0 0.8 copy-start.7

commit v2 on v1

v2 whole, which is shorter than its diff:
```python
import functools

import jax
import jax.numpy as jnp
from jax import lax
from jax.experimental import pallas as pl
from jax.experimental.pallas import tpu as pltpu
from jax.sharding import Mesh
from jax.sharding import PartitionSpec as P

SPAN = 128
DIM = 128
SUPER = 4
STEPS = 8
EACH = 2
PACK = 136
F32 = jnp.float32
BF16 = jnp.bfloat16
EPS = 1e-06
GROUP = ("x", "y", "core")
EVERY = ("z", "x", "y", "core")


def split(x):
    high = x.astype(BF16)
    low = (x - high.astype(F32)).astype(BF16)
    return high, low


def lanes(parts):
    return jnp.concatenate(parts, axis=1)


def rows(parts):
    return jnp.concatenate(parts, axis=0)


def mm(a, b):
    return jnp.dot(a, b, preferred_element_type=F32)


def mm_nt(a, b):
    return lax.dot_general(a, b, (((1,), (1,)), ((), ())), preferred_element_type=F32)


def mm_tn(a, b):
    return lax.dot_general(a, b, (((0,), (0,)), ((), ())), preferred_element_type=F32)


def mm_cat(a_cat, b):
    high, low = split(b)
    depth, width = b.shape
    both = mm(a_cat[:, :depth], lanes([high, low]))
    return both[:, :width] + both[:, width:] + mm(a_cat[:, depth:], high)


def cat(x):
    return lanes(split(x))


def mm3(a, b):
    return mm_cat(cat(a), b)


def inv_sqrt(x):
    x = x + EPS
    guess = lax.rsqrt(x)
    return guess * (1.5 - 0.5 * x * guess * guess)


def index_grids():
    row = lax.broadcasted_iota(jnp.int32, (SPAN, SPAN), 0)
    col = lax.broadcasted_iota(jnp.int32, (SPAN, SPAN), 1)
    return row, col


def lanes_of(pair):
    return pair[:, :SPAN], pair[:, SPAN:]


def mm_wide_cat(left, right):
    depth = right[0].shape[0]
    return mm_wide((left[:, :depth], left[:, depth:]), right)


def mm_wide(left, right):
    width = right[0].shape[1]
    both = mm(left[0], lanes(right))
    return both[:, :width] + both[:, width:] + mm(left[1], right[0])


def unit_lower_inverses(strict, eye, row, col):
    n = range(len(strict))
    halves = [split(strict[i]) for i in n]
    x = [eye - jnp.where((row >> 1) == (col >> 1), strict[i], 0.0) for i in n]
    for level in range(1, 7):
        below = jnp.where(((row >> level) ^ (col >> level)) == 1, 1.0, 0.0).astype(BF16)
        corner = [(halves[i][0] * below, halves[i][1] * below) for i in n]
        x_split = [split(x[i]) for i in n]
        size = 1 << level
        if size < 8:
            part = [mm_wide(x_split[i], corner[i]) for i in n]
            x = [x[i] - mm_wide(split(part[i]), x_split[i]) for i in n]
            continue
        odd = range(size, SPAN, 2 * size)
        lower = [rows([x[i][a : a + size] for a in odd]) for i in n]
        part = [mm_wide(split(lower[i]), corner[i]) for i in n]
        lower = [lower[i] - mm_wide(split(part[i]), x_split[i]) for i in n]
        x = [
            rows([
                piece
                for m, a in enumerate(odd)
                for piece in (x[i][a - size : a], lower[i][m * size : (m + 1) * size])
            ])
            for i in n
        ]
    return x


def keys_kernel(
    kp_ref, xu_ref, yw_ref, n_ref, t_ref, p_ref, c_ref, pcum_ref, suf_ref, total_ref,
    carry, held,
):
    step = pl.program_id(0)
    row, col = index_grids()
    diag = row == col
    eye = jnp.where(diag, 1.0, 0.0).astype(F32)
    unit = eye.astype(BF16)
    each = kp_ref.shape[1]
    cells = [(i, j) for j in range(each) for i in range(SUPER)]
    n = range(len(cells))

    @pl.when(step == 0)
    def _():
        for i in range(SUPER):
            carry[i] = eye
            for j in range(each):
                held[i, j] = lanes([unit, jnp.zeros_like(unit)])

    state = [carry[i] for i in range(SUPER)]
    for c in cells:
        state[c[0]] = mm_cat(held[c], state[c[0]])
    for i in range(SUPER):
        carry[i] = state[i]

    k = [kp_ref[c][:SPAN] for c in cells]
    b_row = [kp_ref[c][SPAN : SPAN + 1].astype(F32) for c in cells]
    gram = [mm_nt(k[i], k[i]) for i in n]
    flipped = [mm_nt(unit, k[i]) for i in n]
    power = [
        jnp.sum(jnp.where(diag, gram[i], 0.0), axis=0, keepdims=True) + EPS for i in n
    ]
    c_row = [b_row[i] / power[i] for i in n]
    strict = [jnp.where(row > col, gram[i] * c_row[i], 0.0) for i in n]
    x = unit_lower_inverses(strict, eye, row, col)
    xu = [split(x[i] * jnp.sqrt(power[i])) for i in n]
    x_split = [split(x[i]) for i in n]
    yw = [mm(lanes(x_split[i]), rows([k[i], k[i]])) for i in n]
    kc = [split(flipped[i] * c_row[i]) for i in n]
    yw_split = [split(yw[i]) for i in n]
    t = [cat(eye - mm_wide(kc[i], yw_split[i])) for i in n]
    for i in n:
        c = cells[i]
        xu_ref[c] = lanes(xu[i])
        yw_ref[c] = lanes(yw_split[i])
        n_ref[c] = cat(mm_wide(kc[i], xu[i]))
        c_ref[c] = c_row[i]
        t_ref[c] = t[i]
        held[c] = t[i]
    for c in cells:
        p_ref[c] = cat(state[c[0]])
        if c[1] < each - 1:
            state[c[0]] = mm_cat(t[cells.index(c)], state[c[0]])

    @pl.when(step == pl.num_programs(0) - 1)
    def _():
        last = [mm_cat(t[n[i - SUPER]], state[i]) for i in range(SUPER)]
        one = mm3(last[1], last[0])
        two = mm3(last[3], last[2])
        pcum_ref[0] = eye
        pcum_ref[1] = last[0]
        pcum_ref[2] = one
        pcum_ref[3] = mm3(last[2], one)
        total_ref[...] = mm3(two, one)
        suf_ref[0] = mm3(two, last[1])
        suf_ref[1] = two
        suf_ref[2] = last[3]
        suf_ref[3] = eye
        suf_ref[4] = last[1]
        suf_ref[5] = last[2]


def suffix_kernel(n_ref, t_ref, suf_ref, m_ref, carry):
    step = pl.program_id(0)
    each = n_ref.shape[1]

    @pl.when(step == 0)
    def _():
        for i in range(SUPER):
            carry[i] = suf_ref[i]

    state = [carry[i] for i in range(SUPER)]
    for j in reversed(range(each)):
        for i in range(SUPER):
            after = cat(state[i])
            pair = lanes_of(after)
            m_ref[i, j] = cat(mm_wide(pair, lanes_of(n_ref[i, j])))
            state[i] = mm_wide(pair, lanes_of(t_ref[i, j]))
    for i in range(SUPER):
        carry[i] = state[i]


def offset_kernel(v_ref, m_ref, total_ref):
    each = v_ref.shape[1]
    parts = []
    for i in range(SUPER):
        for j in range(each):
            v = v_ref[i, j]
            parts.append(mm(m_ref[i, j], rows([v, v])))
    while len(parts) > 1:
        parts = [parts[m] + parts[m + 1] for m in range(0, len(parts), 2)]

    @pl.when(pl.program_id(0) == 0)
    def _():
        total_ref[...] = parts[0]

    @pl.when(pl.program_id(0) > 0)
    def _():
        total_ref[...] += parts[0]


def values_kernel(v_ref, xu_ref, n_ref, t_ref, yu_ref, o_ref, end_ref, carry):
    step = pl.program_id(0)
    count, each = v_ref.shape[:2]
    cells = [(i, j) for j in range(each) for i in range(count)]
    n = range(len(cells))

    @pl.when(step == 0)
    def _():
        carry[...] = jnp.zeros_like(carry)

    v = [v_ref[c] for c in cells]
    doubled = [rows([v[i], v[i]]) for i in n]
    own = [mm(n_ref[cells[i]], doubled[i]) for i in n]
    state = [carry[i] for i in range(count)]
    for m in n:
        c = cells[m]
        o_ref[c] = state[c[0]]
        yu_ref[c] = mm(xu_ref[c], doubled[m])
        state[c[0]] = mm_cat(t_ref[c], state[c[0]]) + own[m]
    for i in range(count):
        carry[i] = state[i]

    @pl.when(step == pl.num_programs(0) - 1)
    def _():
        for i in range(count):
            end_ref[i] = state[i]


def pair_trans_kernel(up_ref, own_ref, other_ref, tup_ref, et_ref, total_ref):
    up = up_ref[0] != 0
    row, col = index_grids()
    eye = jnp.where(row == col, 1.0, 0.0).astype(F32)
    own, other = own_ref[...], other_ref[...]
    upper = jnp.where(up, own, other)
    lower = jnp.where(up, other, own)
    tup_ref[...] = upper
    et_ref[...] = jnp.where(up, other, eye)
    total_ref[...] = mm3(upper, lower)


def quad_trans_kernel(up_ref, own_ref, other_ref, et_ref, tup_ref, et_out_ref):
    up = up_ref[0] != 0
    own, other, et = own_ref[...], other_ref[...], et_ref[...]
    tup_ref[...] = jnp.where(up, own, other)
    et_out_ref[...] = jnp.where(up, mm3(et, other), et)


def pair_offset_kernel(up_ref, own_ref, other_ref, tup_ref, total_ref, eo_ref):
    up = up_ref[0] != 0
    own, other = own_ref[...], other_ref[...]
    lower = jnp.where(up, other, own)
    upper = jnp.where(up, own, other)
    total_ref[...] = mm3(tup_ref[...], lower) + upper
    eo_ref[...] = jnp.where(up, other, 0.0)


def quad_offset_kernel(up_ref, own_ref, other_ref, tup_ref, et_ref, eo_ref, total_ref, eo_out_ref):
    up = up_ref[0] != 0
    own, other, eo = own_ref[...], other_ref[...], eo_ref[...]
    lower = jnp.where(up, other, own)
    upper = jnp.where(up, own, other)
    total_ref[...] = mm3(tup_ref[...], lower) + upper
    eo_out_ref[...] = jnp.where(up, mm3(et_ref[...], other) + eo, eo)


def scores_kernel(q_ref, kp_ref, c_ref, s_ref):
    row, col = index_grids()
    for i in range(SUPER):
        for j in range(q_ref.shape[1]):
            scores = mm_nt(q_ref[i, j], kp_ref[i, j][:SPAN]) * c_ref[i, j]
            s_ref[i, j] = cat(jnp.where(row >= col, scores, 0.0))


def output_kernel(
    up_ref, other_ref, et_ref, eo_ref, pcum_ref, suf_ref, enda_ref, endb_ref,
    q_ref, s_ref, yw_ref, p_ref, yua_ref, yub_ref, oa_ref, ob_ref, out_ref, start,
):
    step = pl.program_id(0)
    each = q_ref.shape[1]
    cells = [(i, j) for j in range(each) for i in range(SUPER)]
    n = range(len(cells))

    @pl.when(step == 0)
    def _():
        eo = eo_ref[...]
        first = jnp.where(up_ref[0] != 0, mm3(et_ref[...], other_ref[...]) + eo, eo)
        start[0] = first
        start[1] = mm3(pcum_ref[1], first) + enda_ref[0]
        middle = mm3(suf_ref[4], enda_ref[0]) + enda_ref[1]
        start[2] = mm3(pcum_ref[2], first) + middle
        start[3] = mm3(pcum_ref[3], first) + (mm3(suf_ref[5], middle) + endb_ref[0])

    def half(low_ref, high_ref, c):
        return low_ref[c] if c[0] < 2 else high_ref[c[0] - 2, c[1]]

    q = [q_ref[c] for c in cells]
    scale = [
        inv_sqrt(jnp.sum(jnp.square(q[i].astype(F32)), axis=1, keepdims=True)) for i in n
    ]
    begin = [split(start[i]) for i in range(SUPER)]
    state = [mm_wide_cat(p_ref[c], begin[c[0]]) + half(oa_ref, ob_ref, c) for c in cells]
    s_split = [split(state[i]) for i in n]
    d_split = [
        split(half(yua_ref, yub_ref, cells[i]) - mm_wide_cat(yw_ref[cells[i]], s_split[i]))
        for i in n
    ]
    for i in n:
        high, low = lanes_of(s_ref[cells[i]])
        left = lanes([q[i], high])
        both = mm(left, rows([lanes(s_split[i]), lanes(d_split[i])]))
        total = both[:, :DIM] + both[:, DIM:] + mm(low, d_split[i][0])
        out_ref[cells[i]] = (total * scale[i]).astype(BF16)


def block(*tail):
    return pl.BlockSpec((SUPER, EACH) + tail, lambda b: (0, b, 0, 0))


def whole(*shape):
    return pl.BlockSpec(shape, lambda b: (0,) * len(shape))


def like(*shape, dtype=F32):
    return jax.ShapeDtypeStruct(shape, dtype)


def cost(passes, nbytes):
    return pl.CostEstimate(
        flops=2 * SUPER * STEPS * passes * SPAN**3, bytes_accessed=nbytes, transcendentals=0
    )


SMEM = pl.BlockSpec(memory_space=pltpu.SMEM)
VMEM = pl.BlockSpec(memory_space=pltpu.VMEM)
MIB = 1 << 20
PARAMS = pltpu.CompilerParams(vmem_limit_bytes=24 * MIB)
FEW = pltpu.CompilerParams(vmem_limit_bytes=2 * MIB)


def small(kernel, outs, *args):
    return pl.pallas_call(
        kernel,
        out_shape=[like(DIM, DIM)] * outs,
        in_specs=[SMEM] + [VMEM] * (len(args) - 1),
        out_specs=[VMEM] * outs,
        compiler_params=FEW,
        cost_estimate=pl.CostEstimate(
            flops=12 * DIM**3, bytes_accessed=65536 * len(args), transcendentals=0
        ),
    )(*args)


def far(*arrays):
    return [pltpu.with_memory_space_constraint(a, pltpu.HBM) for a in arrays]


def exchange(x, distance, size):
    return lax.ppermute(x, "z", [(i, i ^ distance) for i in range(size)])


def shards(query, keys, value, beta):
    depth = lax.axis_size("z")
    z = lax.axis_index("z")
    up1, up2, up4 = [((z >> s) & 1).astype(jnp.int32)[None] for s in (0, 1, 2)]

    def heads_first(array):
        return jnp.transpose(array, (1, 0, 2))

    def to_heads(array):
        return lax.all_to_all(array, GROUP, split_axis=0, concat_axis=0, tiled=True)

    def by_super(array):
        return array.reshape((SUPER, STEPS) + array.shape[1:])

    gates = jnp.pad(beta.T[:, None, :], ((0, 0), (0, PACK - SPAN - 1), (0, 0)))
    packed = jnp.concatenate([heads_first(keys), gates], axis=1)
    mixed = jnp.concatenate([heads_first(value), heads_first(query)], axis=1)
    kp = to_heads(packed)
    mixed, kp = lax.optimization_barrier((mixed, kp))
    vq = by_super(to_heads(mixed))
    kp = by_super(kp)

    full = (SUPER, STEPS)
    half = pltpu.HBM((*full, SPAN, 2 * SPAN), BF16)
    part = pltpu.HBM((*full, SPAN, DIM), F32)
    wide = block(SPAN, 2 * SPAN)
    steps = STEPS // EACH
    xu, yw, nn, t, p, c, pcum, suf, trans = pl.pallas_call(
        keys_kernel,
        grid=(steps,),
        in_specs=[block(PACK, DIM)],
        out_specs=[wide] * 5
        + [block(1, SPAN), whole(4, DIM, DIM), whole(6, DIM, DIM), whole(DIM, DIM)],
        out_shape=[half] * 5
        + [
            pltpu.HBM((*full, 1, SPAN), F32),
            pltpu.HBM((4, DIM, DIM), F32),
            pltpu.HBM((6, DIM, DIM), F32),
            like(DIM, DIM),
        ],
        scratch_shapes=[
            pltpu.VMEM((SUPER, DIM, DIM), F32),
            pltpu.VMEM((SUPER, EACH, SPAN, 2 * SPAN), BF16),
        ],
        compiler_params=PARAMS,
        cost_estimate=cost(47, 11 * MIB),
        name="keys_terms",
    )(kp)
    long = STEPS // 2
    back_block = pl.BlockSpec((SUPER, long, SPAN, 2 * SPAN), lambda b: (0, 1 - b, 0, 0))
    m = pl.pallas_call(
        suffix_kernel,
        grid=(2,),
        in_specs=[back_block, back_block, whole(6, DIM, DIM)],
        out_specs=back_block,
        out_shape=half,
        scratch_shapes=[pltpu.VMEM((SUPER, DIM, DIM), F32)],
        compiler_params=PARAMS,
        cost_estimate=cost(6, 7 * MIB),
        name="suffix_terms",
    )(*far(nn, t, suf))

    tup1, et1, trans2 = small(pair_trans_kernel, 3, up1, trans, exchange(trans, 1, depth))
    vq, trans2, m = lax.optimization_barrier((vq, trans2, m))
    tup2, et2 = small(quad_trans_kernel, 2, up2, trans2, exchange(trans2, 2, depth), et1)

    offset = pl.pallas_call(
        offset_kernel,
        grid=(steps,),
        in_specs=[block(SPAN, DIM), wide],
        out_specs=whole(DIM, DIM),
        out_shape=like(DIM, DIM),
        compiler_params=PARAMS,
        cost_estimate=cost(2, 3 * MIB),
        name="offset_total",
    )(vq, *far(m))

    vq, offset = lax.optimization_barrier((vq, offset))
    second = pl.BlockSpec((SUPER, EACH, SPAN, DIM), lambda b: (0, b, 1, 0))
    scores = pl.pallas_call(
        scores_kernel,
        grid=(steps,),
        in_specs=[second, block(PACK, DIM), block(1, SPAN)],
        out_specs=wide,
        out_shape=half,
        compiler_params=PARAMS,
        cost_estimate=cost(1, 4 * MIB),
        name="scores",
    )(vq, kp, *far(c))
    other, scores = lax.optimization_barrier((exchange(offset, 1, depth), scores))
    off2, eo1 = small(pair_offset_kernel, 2, up1, offset, other, tup1)

    def values_half(index, vq):
        count, each = SUPER // 2, STEPS // 2
        spec = pl.BlockSpec((count, each, SPAN, 2 * SPAN), lambda b: (index, b, 0, 0))
        own = pl.BlockSpec((count, each, SPAN, DIM), lambda b: (0, b, 0, 0))
        piece = pltpu.HBM((count, STEPS, SPAN, DIM), F32)
        return pl.pallas_call(
            values_kernel,
            grid=(STEPS // each,),
            in_specs=[
                pl.BlockSpec((count, each, SPAN, DIM), lambda b: (index, b, 0, 0)),
                spec, spec, spec,
            ],
            out_specs=[own, own, whole(count, DIM, DIM)],
            out_shape=[piece, piece, pltpu.HBM((count, DIM, DIM), F32)],
            scratch_shapes=[pltpu.VMEM((count, DIM, DIM), F32)],
            compiler_params=PARAMS,
            cost_estimate=cost(3, 5 * MIB),
            name="values_terms",
        )(vq, *far(xu, nn, t))

    vq, off2 = lax.optimization_barrier((vq, off2))
    yua, oa, enda = values_half(0, vq)
    other, yua, oa, enda = lax.optimization_barrier((exchange(off2, 2, depth), yua, oa, enda))
    off4, eo2 = small(quad_offset_kernel, 2, up2, off2, other, tup2, et1, eo1)
    vq, off4 = lax.optimization_barrier((vq, off4))
    yub, ob, endb = values_half(1, vq)
    other = exchange(off4, 4, depth)

    piece = pl.BlockSpec((SUPER // 2, EACH, SPAN, DIM), lambda b: (0, b, 0, 0))
    out = pl.pallas_call(
        output_kernel,
        grid=(STEPS // EACH,),
        in_specs=[
            SMEM, whole(DIM, DIM), whole(DIM, DIM), whole(DIM, DIM),
            whole(4, DIM, DIM), whole(6, DIM, DIM), whole(2, DIM, DIM), whole(2, DIM, DIM),
            second, wide, wide, wide, piece, piece, piece, piece,
        ],
        out_specs=block(SPAN, DIM),
        out_shape=like(*full, SPAN, DIM, dtype=BF16),
        scratch_shapes=[pltpu.VMEM((SUPER, DIM, DIM), F32)],
        compiler_params=PARAMS,
        cost_estimate=cost(12, 11 * MIB),
        name="mix_output",
    )(
        up4, other, et2, eo2, *far(pcum, suf, enda, endb),
        vq, *far(scores, yw, p, yua, yub, oa, ob),
    )
    back = to_heads(out.reshape(SUPER * STEPS, SPAN, DIM))
    return jnp.transpose(back, (1, 0, 2))


def solution(mesh):
    fine = Mesh(mesh.devices.reshape(8, 4, 4, 2), EVERY)
    placed = (P(EVERY, None, None), P(EVERY, None, None), P(EVERY, None, None), P(EVERY, None))
    return jax.shard_map(
        shards,
        mesh=fine,
        in_specs=placed,
        out_specs=P(EVERY, None, None),
        check_vma=False,
    )
```

time: 159 us -> 119 us (0.75)
  waiting for transfers between devices: 34.1 us -> 19.1 us
  local copies, waits for them, and re-layouts: 17.7 us -> 6.35 us
  blocking collectives: 27.3 us -> 21.7 us
  Pallas kernels: 49.7 us -> 44.2 us
  starting transfers between devices: 28.1 us -> 24.6 us
    unnamed x34 -> x2, local copies, waits for them, and re-layouts: 15.4 us -> 2.34 us
    all_to_all x3 -> x2, waiting for transfers between devices: 31.8 us -> 19.1 us  [to_heads(): return lax.all_to_all(array, GROUP, split_axis=0, concat_axis=0, tiled=True)]
    pallas_call x4, Pallas kernels: 6.89 us -> 0.73 us  [small(): pl.pallas_call(kernel, out_shape=[like(DIM, DIM)] * outs, in_specs=[SMEM]...]
    all_to_all x1, blocking collectives: 27.3 us -> 21.7 us  [to_heads(): return lax.all_to_all(array, GROUP, split_axis=0, concat_axis=0, tiled=True)]
    all_to_all x3 -> x2, starting transfers between devices: 16.5 us -> 12.5 us  [to_heads(): return lax.all_to_all(array, GROUP, split_axis=0, concat_axis=0, tiled=True)]
    transpose x0 -> x1, local copies, waits for them, and re-layouts: none -> 2.36 us  [heads_first(): return jnp.transpose(array, (1, 0, 2))]
    ppermute x5, waiting for transfers between devices: 2.37 us -> 0.07 us  [exchange(): return lax.ppermute(x, 'z', [(i, i ^ distance) for i in range(size)])]
    pallas_call x3 -> x7, Pallas kernels: 42.8 us -> 43.4 us  [the longest x1 16.5 us: shards(): pl.pallas_call(keys_kernel, grid=(steps,), in_specs=[block(PACK, DIM)], o...]
  transfers between devices with their start and end apart: 8 -> 7, of which waited for: 4 -> 3; matrix products, arithmetic and copies ran while one was open for 2% -> 3% of each run, Pallas kernels for 26% -> 28%
where the time goes in v2:
time: 119 us
  Pallas kernels  44.2 us (37%)
  starting transfers between devices  24.6 us (21%)
  blocking collectives  21.7 us (18%)
  waiting for transfers between devices  19.1 us (16%)
  local copies, waits for them, and re-layouts  6.35 us (5%)
  other arithmetic  2.67 us (2%)
    all_to_all x1, blocking collectives, to_heads(): return lax.all_to_all(array, GROUP, split_axis=0, concat_axis=0, tiled=True)  21.7 us
    all_to_all x2, waiting for transfers between devices, to_heads(): return lax.all_to_all(array, GROUP, split_axis=0, concat_axis=0, tiled=True)  19.1 us
    pallas_call x1, Pallas kernels, shards(): pl.pallas_call(keys_kernel, grid=(steps,), in_specs=[block(PACK, DIM)], o...  16.5 us
    all_to_all x2, starting transfers between devices, to_heads(): return lax.all_to_all(array, GROUP, split_axis=0, concat_axis=0, tiled=True)  12.5 us
    ppermute x5, starting transfers between devices, exchange(): return lax.ppermute(x, 'z', [(i, i ^ distance) for i in range(size)])  12.1 us
    pallas_call x2, Pallas kernels, values_half(): pl.pallas_call(values_kernel, grid=(STEPS // each,), in_specs=[pl.BlockSp...  8.54 us
    pallas_call x1, Pallas kernels, shards(): pl.pallas_call(output_kernel, grid=(STEPS // EACH,), in_specs=[SMEM, whol...  7.07 us
    pallas_call x1, Pallas kernels, shards(): pl.pallas_call(suffix_kernel, grid=(2,), in_specs=[back_block, back_block...  4.61 us
  transfers between devices with their start and end apart: 7, of which 3 were waited for; matrix products, arithmetic and copies ran while one was open for 3% of the time, Pallas kernels for 28%

profile of v2, /device:TPU:1, one launch (start us, length us, event | category | flops | bytes accessed | tf_op | source)
XLA Modules:
  0.0 118.7 jit_solution(1112488035014495158)
XLA Ops:
  0.0 0.7 copy.17
  0.7 1.6 %copy.21 = bf16[128,32,128]{2,0,1:T(8,128)(2,1)S(1)} copy(bf16[128,32,128]{2,1,0:T(8,128)(2,1)} %param.5) | data formatting | bytes 2097152 | tf_op args[1]
  2.4 1.1 fusion.1
  3.5 8.6 %all-to-all-start = ((bf16[32,136,128]{2,1,0:T(8,128)(2,1)}), bf16[32,136,128]{2,1,0:T(8,128)(2,1)S(1)}, u32[]{:S(2)}, u32[]{:S(2)}) async-start(bf16[32,136,128]{2,1,0:T(8,128)(2,1)} %fusion.1), calls=%async_computation | async-start | bytes 2228224 | tf_op jit(solution)/shard_map/all_to_all | solution.py:401
  12.1 2.4 %copy_bitcast_fusion.1 = (bf16[32,128,128]{2,1,0:T(8,128)(2,1)S(1)}, bf16[32,128,128]{2,1,0:T(8,128)(2,1)S(1)}) fusion(bf16[128,32,128]{2,1,0:T(8,128)(2,1)} %param.4, bf16[128,32,128]{2,1,0:T(8,128)(2,1)} %param.6), kind=kLoop, calls=%fused_computation.5 | loop fusion | bytes 4194304 | tf_op jit(solution)/shard_map/transpose | solution.py:398
  14.4 1.6 %pad_maximum_fusion = bf16[32,256,128]{2,1,0:T(8,128)(2,1)} fusion(bf16[32,128,128]{2,1,0:T(8,128)(2,1)S(1)} %get-tuple-element.87, bf16[32,128,128]{2,1,0:T(8,128)(2,1)S(1)} %get-tuple-element.88), kind=kLoop, calls=%fused_computation.2 | loop fusion | flops 4194304 | bytes 4194304 | tf_op jit(solution)/shard_map/concatenate | solution.py:408
  16.0 13.7 %all-to-all-done = bf16[32,136,128]{2,1,0:T(8,128)(2,1)S(1)} async-done(((bf16[32,136,128]{2,1,0:T(8,128)(2,1)}), bf16[32,136,128]{2,1,0:T(8,128)(2,1)S(1)}, u32[]{:S(2)}, u32[]{:S(2)}) %all-to-all-start) | async-done | bytes 1114144 | tf_op jit(solution)/shard_map/all_to_all | solution.py:401
  29.7 3.9 %all-to-all-start.1 = ((bf16[32,256,128]{2,1,0:T(8,128)(2,1)}), bf16[32,256,128]{2,1,0:T(8,128)(2,1)S(1)}, u32[]{:S(2)}, u32[]{:S(2)}) async-start(bf16[32,256,128]{2,1,0:T(8,128)(2,1)} %pad_maximum_fusion), calls=%async_computation.1 | async-start | bytes 4194304 | tf_op jit(solution)/shard_map/all_to_all | solution.py:401
  33.6 16.5 %keys_terms.1 = (bf16[4,8,128,256]{3,2,1,0:T(8,128)(2,1)}, bf16[4,8,128,256]{3,2,1,0:T(8,128)(2,1)}, bf16[4,8,128,256]{3,2,1,0:T(8,128)(2,1)}, bf16[4,8,128,256]...) custom-call(bf16[4,8,136,128]{3,2,1,0:T(8,128)(2,1)S(1)} %bitcast.22), custom_call_target="tpu_custom_call" | custom-call | flops 6308233216 | bytes 11534336 | tf_op jit(solution)/shard_map/keys_terms/pallas_call | solution.py:419
  50.1 1.7 %collective-permute-start = (f32[128,128]{1,0:T(8,128)S(1)}, f32[128,128]{1,0:T(8,128)S(1)}, u32[]{:S(2)}, u32[]{:S(2)}) collective-permute-start(f32[128,128]{1,0:T(8,128)S(1)} %get-tuple-element.48.own_ref), channel_id=1, source_target_pairs={{0,32},{32,0},{64,96},{96,64},{128,160},{160,128},{192,224},{224,1... | collective-permute-start | bytes 196616 | tf_op jit(solution)/shard_map/ppermute | solution.py:389
  51.8 4.6 %suffix_terms.1.m_ref = bf16[4,8,128,256]{3,2,1,0:T(8,128)(2,1)} custom-call(bf16[4,8,128,256]{3,2,1,0:T(8,128)(2,1)} %get-tuple-element.50.n_ref, bf16[4,8,128,256]{3,2,1,0:T(8,128)(2,1)} %get-tuple-element.51.t_ref, f32[6,128,128]{2,1,0:T(8,128)} %get-tuple-element.52.suf_ref), custom_call_target="tpu_custom_call" | custom-call | flops 805306368 | bytes 7340032 | tf_op jit(solution)/shard_map/suffix_terms/pallas_call | solution.py:442
  56.4 0.0 collective-permute-done.other_ref
  56.4 0.2 shard_map.46
  56.6 5.3 %all-to-all-done.1 = bf16[32,256,128]{2,1,0:T(8,128)(2,1)S(1)} async-done(((bf16[32,256,128]{2,1,0:T(8,128)(2,1)}), bf16[32,256,128]{2,1,0:T(8,128)(2,1)S(1)}, u32[]{:S(2)}, u32[]{:S(2)}) %all-to-all-start.1) | async-done | bytes 2097184 | tf_op jit(solution)/shard_map/all_to_all | solution.py:401
  61.9 3.1 %offset_total.1.own_ref = f32[128,128]{1,0:T(8,128)S(1)} custom-call(bf16[4,8,256,128]{3,2,1,0:T(8,128)(2,1)S(1)} %bitcast.17, bf16[4,8,128,256]{3,2,1,0:T(8,128)(2,1)} %suffix_terms.1.m_ref), custom_call_target="tpu_custom_call" | custom-call | flops 268435456 | bytes 3145728 | tf_op jit(solution)/shard_map/offset_total/pallas_call | solution.py:458
  65.1 1.7 %collective-permute-start.1 = (f32[128,128]{1,0:T(8,128)S(1)}, f32[128,128]{1,0:T(8,128)S(1)}, u32[]{:S(2)}, u32[]{:S(2)}) collective-permute-start(f32[128,128]{1,0:T(8,128)S(1)} %offset_total.1.own_ref), channel_id=1, source_target_pairs={{0,32},{32,0},{64,96},{96,64},{128,160},{160,128},{192,224},{224,1... | collective-permute-start | bytes 196616 | tf_op jit(solution)/shard_map/ppermute | solution.py:389
  66.8 3.0 %collective-permute-start.3 = (f32[128,128]{1,0:T(8,128)S(1)}, f32[128,128]{1,0:T(8,128)S(1)}, u32[]{:S(2)}, u32[]{:S(2)}) collective-permute-start(f32[128,128]{1,0:T(8,128)S(1)} %get-tuple-element.68.own_ref), channel_id=1, source_target_pairs={{0,64},{32,96},{64,0},{96,32},{128,192},{160,224},{192,128},{224,1... | collective-permute-start | bytes 196616 | tf_op jit(solution)/shard_map/ppermute | solution.py:389
  69.8 3.7 %scores.1.s_ref = bf16[4,8,128,256]{3,2,1,0:T(8,128)(2,1)} custom-call(bf16[4,8,256,128]{3,2,1,0:T(8,128)(2,1)S(1)} %bitcast.18, bf16[4,8,136,128]{3,2,1,0:T(8,128)(2,1)S(1)} %bitcast.23, f32[4,8,1,128]{3,2,1,0:T(1,128)} %get-tuple-element.57.c_ref), custom_call_target="tpu_custom_call" | custom-call | flops 134217728 | bytes 4194304 | tf_op jit(solution)/shard_map/scores/pallas_call | solution.py:471
  73.4 0.0 collective-permute-done.1.other_ref
  73.4 0.2 shard_map.47
  73.6 0.1 collective-permute-start.2
  73.7 0.0 collective-permute-done.3.other_ref
  73.7 0.2 shard_map.48
  73.9 4.3 %values_terms.2 = (f32[2,8,128,128]{3,2,1,0:T(8,128)}, f32[2,8,128,128]{3,2,1,0:T(8,128)}, f32[2,128,128]{2,1,0:T(8,128)}) custom-call(bf16[4,8,256,128]{3,2,1,0:T(8,128)(2,1)S(1)} %bitcast.19, bf16[4,8,128,256]{3,2,1,0:T(8,128)(2,1)} %get-tuple-element.63.xu_ref, bf16[4,8,128,256]{3,2,1,0:T(8,128)(2,1)} %get-tuple-element.50.n_ref, ...), custom_call_target="tpu_custom_call" | custom-call | flops 402653184 | bytes 5242880 | tf_op jit(solution)/shard_map/values_terms/pallas_call | solution.py:489
  78.2 0.1 collective-permute-done.2.other_ref
  78.2 0.2 shard_map.49
  78.5 5.6 %collective-permute-start.4 = (f32[128,128]{1,0:T(8,128)S(1)}, f32[128,128]{1,0:T(8,128)S(1)}, u32[]{:S(2)}, u32[]{:S(2)}) collective-permute-start(f32[128,128]{1,0:T(8,128)S(1)} %get-tuple-element.73), channel_id=1, source_target_pairs={{0,128},{32,160},{64,192},{96,224},{128,0},{160,32},{192,64},{224,... | collective-permute-start | bytes 196616 | tf_op jit(solution)/shard_map/ppermute | solution.py:389
  84.0 4.3 %values_terms.3 = (f32[2,8,128,128]{3,2,1,0:T(8,128)}, f32[2,8,128,128]{3,2,1,0:T(8,128)}, f32[2,128,128]{2,1,0:T(8,128)}) custom-call(bf16[4,8,256,128]{3,2,1,0:T(8,128)(2,1)S(1)} %bitcast.20, bf16[4,8,128,256]{3,2,1,0:T(8,128)(2,1)} %get-tuple-element.63.xu_ref, bf16[4,8,128,256]{3,2,1,0:T(8,128)(2,1)} %get-tuple-element.50.n_ref, ...), custom_call_target="tpu_custom_call" | custom-call | flops 402653184 | bytes 5242880 | tf_op jit(solution)/shard_map/values_terms/pallas_call | solution.py:489
  88.3 0.0 collective-permute-done.4.other_ref
  88.3 7.1 %mix_output.1 = bf16[4,8,128,128]{3,2,1,0:T(8,128)(2,1)S(1)} custom-call(s32[1]{0:T(128)} %bitcast.up_ref, f32[128,128]{1,0:T(8,128)S(1)} %collective-permute-done.4.other_ref, f32[128,128]{1,0:T(8,128)S(1)} %get-tuple-element.74.et_ref, f32[128,128]{1,0:T(8,128)S(1)} %get-tuple-element.75.eo_ref, f32[4,128,128]{2,1,0:T(8,128)} %get-tuple-element.76.pcum_ref, ...), custom_call_target="tpu_custom_call" | custom-call | flops 1610612736 | bytes 11534336 | tf_op jit(solution)/shard_map/mix_output/pallas_call | solution.py:513
  95.4 21.7 %all_to_all.15 = bf16[32,128,128]{2,1,0:T(8,128)(2,1)S(1)} all-to-all(bf16[32,128,128]{2,1,0:T(8,128)(2,1)S(1)} %bitcast.24), channel_id=1, replica_groups=mesh['z'=8,'x'=4,'y'=4,'core'=2] {'x','y','core'}, dimensions={0} | all-to-all | bytes 2097152 | tf_op jit(solution)/shard_map/all_to_all | solution.py:401
  117.1 1.6 %copy.16 = bf16[128,32,128]{2,1,0:T(8,128)(2,1)} copy(bf16[128,32,128]{2,0,1:T(8,128)(2,1)S(1)} %bitcast.26) | data formatting | bytes 2097152 | tf_op jit(solution)/shard_map/transpose | solution.py:532
Async XLA Ops:
  3.5 26.2 %all-to-all-start = ((bf16[32,136,128]{2,1,0:T(8,128)(2,1)}), bf16[32,136,128]{2,1,0:T(8,128)(2,1)S(1)}, u32[]{:S(2)}, u32[]{:S(2)}) async-start(bf16[32,136,128]{2,1,0:T(8,128)(2,1)} %fusion.1), calls=%async_computation | async-start | bytes 2228224 | tf_op jit(solution)/shard_map/all_to_all | solution.py:401
  29.7 32.2 %all-to-all-start.1 = ((bf16[32,256,128]{2,1,0:T(8,128)(2,1)}), bf16[32,256,128]{2,1,0:T(8,128)(2,1)S(1)}, u32[]{:S(2)}, u32[]{:S(2)}) async-start(bf16[32,256,128]{2,1,0:T(8,128)(2,1)} %pad_maximum_fusion), calls=%async_computation.1 | async-start | bytes 4194304 | tf_op jit(solution)/shard_map/all_to_all | solution.py:401
  50.1 6.3 %collective-permute-start = (f32[128,128]{1,0:T(8,128)S(1)}, f32[128,128]{1,0:T(8,128)S(1)}, u32[]{:S(2)}, u32[]{:S(2)}) collective-permute-start(f32[128,128]{1,0:T(8,128)S(1)} %get-tuple-element.48.own_ref), channel_id=1, source_target_pairs={{0,32},{32,0},{64,96},{96,64},{128,160},{160,128},{192,224},{224,1... | collective-permute-start | bytes 196616 | tf_op jit(solution)/shard_map/ppermute | solution.py:389
  65.1 8.4 %collective-permute-start.1 = (f32[128,128]{1,0:T(8,128)S(1)}, f32[128,128]{1,0:T(8,128)S(1)}, u32[]{:S(2)}, u32[]{:S(2)}) collective-permute-start(f32[128,128]{1,0:T(8,128)S(1)} %offset_total.1.own_ref), channel_id=1, source_target_pairs={{0,32},{32,0},{64,96},{96,64},{128,160},{160,128},{192,224},{224,1... | collective-permute-start | bytes 196616 | tf_op jit(solution)/shard_map/ppermute | solution.py:389
  66.8 7.0 %collective-permute-start.3 = (f32[128,128]{1,0:T(8,128)S(1)}, f32[128,128]{1,0:T(8,128)S(1)}, u32[]{:S(2)}, u32[]{:S(2)}) collective-permute-start(f32[128,128]{1,0:T(8,128)S(1)} %get-tuple-element.68.own_ref), channel_id=1, source_target_pairs={{0,64},{32,96},{64,0},{96,32},{128,192},{160,224},{192,128},{224,1... | collective-permute-start | bytes 196616 | tf_op jit(solution)/shard_map/ppermute | solution.py:389
  73.6 4.6 %collective-permute-start.2 = (f32[128,128]{1,0:T(8,128)S(1)}, f32[128,128]{1,0:T(8,128)S(1)}, u32[]{:S(2)}, u32[]{:S(2)}) collective-permute-start(f32[128,128]{1,0:T(8,128)S(1)} %get-tuple-element.62.own_ref), channel_id=1, source_target_pairs={{0,64},{32,96},{64,0},{96,32},{128,192},{160,224},{192,128},{224,1... | collective-permute-start | bytes 196616 | tf_op jit(solution)/shard_map/ppermute | solution.py:389
  78.5 9.9 %collective-permute-start.4 = (f32[128,128]{1,0:T(8,128)S(1)}, f32[128,128]{1,0:T(8,128)S(1)}, u32[]{:S(2)}, u32[]{:S(2)}) collective-permute-start(f32[128,128]{1,0:T(8,128)S(1)} %get-tuple-element.73), channel_id=1, source_target_pairs={{0,128},{32,160},{64,192},{96,224},{128,0},{160,32},{192,64},{224,... | collective-permute-start | bytes 196616 | tf_op jit(solution)/shard_map/ppermute | solution.py:389

commit v3 on v2

--- a/solution.py
+++ b/solution.py
@@ -13,6 +13,7 @@
 SUPER = 4
 STEPS = 8
 EACH = 2
+LONG = 4
 PACK = 136
 F32 = jnp.float32
 BF16 = jnp.bfloat16
@@ -303,7 +304,7 @@
 
 
 def output_kernel(
-    up_ref, other_ref, et_ref, eo_ref, pcum_ref, suf_ref, enda_ref, endb_ref,
+    up_ref, other_ref, et_ref, eo_ref, pcum_ref, suf_ref, end_ref,
     q_ref, s_ref, yw_ref, p_ref, yua_ref, yub_ref, oa_ref, ob_ref, out_ref, start,
 ):
     step = pl.program_id(0)
@@ -316,13 +317,13 @@
         eo = eo_ref[...]
         first = jnp.where(up_ref[0] != 0, mm3(et_ref[...], other_ref[...]) + eo, eo)
         start[0] = first
-        start[1] = mm3(pcum_ref[1], first) + enda_ref[0]
-        middle = mm3(suf_ref[4], enda_ref[0]) + enda_ref[1]
+        start[1] = mm3(pcum_ref[1], first) + end_ref[0]
+        middle = mm3(suf_ref[4], end_ref[0]) + end_ref[1]
         start[2] = mm3(pcum_ref[2], first) + middle
-        start[3] = mm3(pcum_ref[3], first) + (mm3(suf_ref[5], middle) + endb_ref[0])
+        start[3] = mm3(pcum_ref[3], first) + (mm3(suf_ref[5], middle) + end_ref[2])
 
     def half(low_ref, high_ref, c):
-        return low_ref[c] if c[0] < 2 else high_ref[c[0] - 2, c[1]]
+        return low_ref[c] if c[0] < SUPER - 1 else high_ref[0, c[1]]
 
     q = [q_ref[c] for c in cells]
     scale = [
@@ -455,10 +456,13 @@
     vq, trans2, m = lax.optimization_barrier((vq, trans2, m))
     tup2, et2 = small(quad_trans_kernel, 2, up2, trans2, exchange(trans2, 2, depth), et1)
 
+    def half_of(*shape, place=0):
+        return pl.BlockSpec((SUPER, LONG) + shape, lambda b: (0, b, place, 0))
+
     offset = pl.pallas_call(
         offset_kernel,
-        grid=(steps,),
-        in_specs=[block(SPAN, DIM), wide],
+        grid=(STEPS // LONG,),
+        in_specs=[half_of(SPAN, DIM), half_of(SPAN, 2 * SPAN)],
         out_specs=whole(DIM, DIM),
         out_shape=like(DIM, DIM),
         compiler_params=PARAMS,
@@ -467,12 +471,11 @@
     )(vq, *far(m))
 
     vq, offset = lax.optimization_barrier((vq, offset))
-    second = pl.BlockSpec((SUPER, EACH, SPAN, DIM), lambda b: (0, b, 1, 0))
     scores = pl.pallas_call(
         scores_kernel,
-        grid=(steps,),
-        in_specs=[second, block(PACK, DIM), block(1, SPAN)],
-        out_specs=wide,
+        grid=(STEPS // LONG,),
+        in_specs=[half_of(SPAN, DIM, place=1), half_of(PACK, DIM), half_of(1, SPAN)],
+        out_specs=half_of(SPAN, 2 * SPAN),
         out_shape=half,
         compiler_params=PARAMS,
         cost_estimate=cost(1, 4 * MIB),
@@ -481,52 +484,56 @@
     other, scores = lax.optimization_barrier((exchange(offset, 1, depth), scores))
     off2, eo1 = small(pair_offset_kernel, 2, up1, offset, other, tup1)
 
-    def values_half(index, vq):
-        count, each = SUPER // 2, STEPS // 2
-        spec = pl.BlockSpec((count, each, SPAN, 2 * SPAN), lambda b: (index, b, 0, 0))
-        own = pl.BlockSpec((count, each, SPAN, DIM), lambda b: (0, b, 0, 0))
-        piece = pltpu.HBM((count, STEPS, SPAN, DIM), F32)
+    def values_part(count, place, vq, pin):
+        spec = pl.BlockSpec((count, LONG, SPAN, 2 * SPAN), lambda b: (place, b, 0, 0))
+        own = pl.BlockSpec((count, LONG, SPAN, DIM), lambda b: (0, b, 0, 0))
+        make = pltpu.HBM if pin else jax.ShapeDtypeStruct
+        piece = make((count, STEPS, SPAN, DIM), F32)
         return pl.pallas_call(
             values_kernel,
-            grid=(STEPS // each,),
+            grid=(STEPS // LONG,),
             in_specs=[
-                pl.BlockSpec((count, each, SPAN, DIM), lambda b: (index, b, 0, 0)),
+                pl.BlockSpec((count, LONG, SPAN, DIM), lambda b: (place, b, 0, 0)),
                 spec, spec, spec,
             ],
             out_specs=[own, own, whole(count, DIM, DIM)],
-            out_shape=[piece, piece, pltpu.HBM((count, DIM, DIM), F32)],
+            out_shape=[piece, piece, make((count, DIM, DIM), F32)],
             scratch_shapes=[pltpu.VMEM((count, DIM, DIM), F32)],
             compiler_params=PARAMS,
-            cost_estimate=cost(3, 5 * MIB),
+            cost_estimate=cost(count, 3 * count * MIB),
             name="values_terms",
         )(vq, *far(xu, nn, t))
 
     vq, off2 = lax.optimization_barrier((vq, off2))
-    yua, oa, enda = values_half(0, vq)
-    other, yua, oa, enda = lax.optimization_barrier((exchange(off2, 2, depth), yua, oa, enda))
+    yub, ob, _ = values_part(1, SUPER - 1, vq, True)
+    other, yub, ob = lax.optimization_barrier((exchange(off2, 2, depth), yub, ob))
     off4, eo2 = small(quad_offset_kernel, 2, up2, off2, other, tup2, et1, eo1)
     vq, off4 = lax.optimization_barrier((vq, off4))
-    yub, ob, endb = values_half(1, vq)
+    yua, oa, end = values_part(SUPER - 1, 0, vq, False)
     other = exchange(off4, 4, depth)
 
-    piece = pl.BlockSpec((SUPER // 2, EACH, SPAN, DIM), lambda b: (0, b, 0, 0))
+    def all_of(count, *shape, place=0):
+        return pl.BlockSpec((count, STEPS) + shape, lambda b: (0, 0, place, 0))
+
+    most, one = all_of(SUPER - 1, SPAN, DIM), all_of(1, SPAN, DIM)
+    pair = all_of(SUPER, SPAN, 2 * SPAN)
     out = pl.pallas_call(
         output_kernel,
-        grid=(STEPS // EACH,),
+        grid=(1,),
         in_specs=[
             SMEM, whole(DIM, DIM), whole(DIM, DIM), whole(DIM, DIM),
-            whole(4, DIM, DIM), whole(6, DIM, DIM), whole(2, DIM, DIM), whole(2, DIM, DIM),
-            second, wide, wide, wide, piece, piece, piece, piece,
+            whole(4, DIM, DIM), whole(6, DIM, DIM), whole(3, DIM, DIM),
+            all_of(SUPER, SPAN, DIM, place=1), pair, pair, pair, most, one, most, one,
         ],
-        out_specs=block(SPAN, DIM),
+        out_specs=all_of(SUPER, SPAN, DIM),
         out_shape=like(*full, SPAN, DIM, dtype=BF16),
         scratch_shapes=[pltpu.VMEM((SUPER, DIM, DIM), F32)],
-        compiler_params=PARAMS,
+        compiler_params=pltpu.CompilerParams(vmem_limit_bytes=40 * MIB),
         cost_estimate=cost(12, 11 * MIB),
         name="mix_output",
     )(
-        up4, other, et2, eo2, *far(pcum, suf, enda, endb),
-        vq, *far(scores, yw, p, yua, yub, oa, ob),
+        up4, other, et2, eo2, *far(pcum, suf), end,
+        vq, scores, yw, p, yua, yub, oa, ob,
     )
     back = to_heads(out.reshape(SUPER * STEPS, SPAN, DIM))
     return jnp.transpose(back, (1, 0, 2))

time: 119 us -> 115 us (0.966)
  Pallas kernels: 44.2 us -> 38.8 us
  waiting for transfers between devices: 19.1 us -> 21.3 us
  local copies, waits for them, and re-layouts: 6.35 us -> 5.14 us
    pallas_call x5, Pallas kernels: 22.4 us -> 16.9 us  [the longest x2 7.64 us: values_part(): pl.pallas_call(values_kernel, grid=(STEPS // LONG,), in_specs=[pl.BlockSp...]
    transpose x1, local copies, waits for them, and re-layouts: 2.36 us -> 0.81 us  [heads_first(): return jnp.transpose(array, (1, 0, 2))]
    all_to_all x2, waiting for transfers between devices: 19.1 us -> 20.5 us  [to_heads(): return lax.all_to_all(array, GROUP, split_axis=0, concat_axis=0, tiled=True)]
    unnamed x2 -> x16, local copies, waits for them, and re-layouts: 2.34 us -> 2.68 us
  transfers between devices with their start and end apart: 7 -> 7, of which waited for: 3 -> 3; matrix products, arithmetic and copies ran while one was open for 3% -> 2% of each run, Pallas kernels for 28% -> 28%
where the time goes in v3:
time: 115 us; the launch traced here: 114 us
  Pallas kernels  38.8 us (34%)
  starting transfers between devices  23.9 us (21%)
  blocking collectives  22.4 us (19%)
  waiting for transfers between devices  21.3 us (19%)
  local copies, waits for them, and re-layouts  5.14 us (4%)
  other arithmetic  2.68 us (2%)
    all_to_all x1, blocking collectives, to_heads(): return lax.all_to_all(array, GROUP, split_axis=0, concat_axis=0, tiled=True)  22.4 us
    all_to_all x2, waiting for transfers between devices, to_heads(): return lax.all_to_all(array, GROUP, split_axis=0, concat_axis=0, tiled=True)  20.5 us
    pallas_call x1, Pallas kernels, shards(): pl.pallas_call(keys_kernel, grid=(steps,), in_specs=[block(PACK, DIM)], o...  16.4 us
    all_to_all x2, starting transfers between devices, to_heads(): return lax.all_to_all(array, GROUP, split_axis=0, concat_axis=0, tiled=True)  12.5 us
    ppermute x5, starting transfers between devices, exchange(): return lax.ppermute(x, 'z', [(i, i ^ distance) for i in range(size)])  11.4 us
    pallas_call x2, Pallas kernels, values_part(): pl.pallas_call(values_kernel, grid=(STEPS // LONG,), in_specs=[pl.BlockSp...  7.64 us
    pallas_call x1, Pallas kernels, shards(): pl.pallas_call(suffix_kernel, grid=(2,), in_specs=[back_block, back_block...  4.63 us
    pallas_call x1, Pallas kernels, shards(): pl.pallas_call(output_kernel, grid=(1,), in_specs=[SMEM, whole(DIM, DIM),...  4.37 us
  transfers between devices with their start and end apart: 7, of which 3 were waited for; matrix products, arithmetic and copies ran while one was open for 2% of the time, Pallas kernels for 28%

profile of v3, /device:TPU:1, one launch (start us, length us, event | category | flops | bytes accessed | tf_op | source)
XLA Modules:
  0.0 114.4 jit_solution(11586876394257578222)
XLA Ops:
  0.0 0.7 copy.17
  0.7 1.6 %copy.21 = bf16[128,32,128]{2,0,1:T(8,128)(2,1)S(1)} copy(bf16[128,32,128]{2,1,0:T(8,128)(2,1)} %param.5) | data formatting | bytes 2097152 | tf_op args[1]
  2.4 0.0 copy-start.5
  2.4 0.0 copy-start.6
  2.4 1.1 fusion.1
  3.5 8.6 %all-to-all-start = ((bf16[32,136,128]{2,1,0:T(8,128)(2,1)}), bf16[32,136,128]{2,1,0:T(8,128)(2,1)S(1)}, u32[]{:S(2)}, u32[]{:S(2)}) async-start(bf16[32,136,128]{2,1,0:T(8,128)(2,1)} %fusion.1), calls=%async_computation | async-start | bytes 2228224 | tf_op jit(solution)/shard_map/all_to_all | solution.py:402
  12.1 0.0 copy-done.5
  12.1 0.0 copy-done.6
  12.1 0.8 copy_bitcast_fusion.1
  12.9 1.6 %pad_maximum_fusion = bf16[32,256,128]{2,1,0:T(8,128)(2,1)} fusion(bf16[32,128,128]{2,1,0:T(8,128)(2,1)S(1)} %get-tuple-element.83, bf16[32,128,128]{2,1,0:T(8,128)(2,1)S(1)} %get-tuple-element.84), kind=kLoop, calls=%fused_computation.2 | loop fusion | flops 4194304 | bytes 4194304 | tf_op jit(solution)/shard_map/concatenate | solution.py:409
  14.5 15.2 %all-to-all-done = bf16[32,136,128]{2,1,0:T(8,128)(2,1)S(1)} async-done(((bf16[32,136,128]{2,1,0:T(8,128)(2,1)}), bf16[32,136,128]{2,1,0:T(8,128)(2,1)S(1)}, u32[]{:S(2)}, u32[]{:S(2)}) %all-to-all-start) | async-done | bytes 1114144 | tf_op jit(solution)/shard_map/all_to_all | solution.py:402
  29.7 3.9 %all-to-all-start.1 = ((bf16[32,256,128]{2,1,0:T(8,128)(2,1)}), bf16[32,256,128]{2,1,0:T(8,128)(2,1)S(1)}, u32[]{:S(2)}, u32[]{:S(2)}) async-start(bf16[32,256,128]{2,1,0:T(8,128)(2,1)} %pad_maximum_fusion), calls=%async_computation.1 | async-start | bytes 4194304 | tf_op jit(solution)/shard_map/all_to_all | solution.py:402
  33.7 16.4 %keys_terms.1 = (bf16[4,8,128,256]{3,2,1,0:T(8,128)(2,1)}, bf16[4,8,128,256]{3,2,1,0:T(8,128)(2,1)}, bf16[4,8,128,256]{3,2,1,0:T(8,128)(2,1)}, bf16[4,8,128,256]...) custom-call(bf16[4,8,136,128]{3,2,1,0:T(8,128)(2,1)S(1)} %bitcast.22), custom_call_target="tpu_custom_call" | custom-call | flops 6308233216 | bytes 11534336 | tf_op jit(solution)/shard_map/keys_terms/pallas_call | solution.py:420
  50.1 1.7 %collective-permute-start = (f32[128,128]{1,0:T(8,128)S(1)}, f32[128,128]{1,0:T(8,128)S(1)}, u32[]{:S(2)}, u32[]{:S(2)}) collective-permute-start(f32[128,128]{1,0:T(8,128)S(1)} %get-tuple-element.46.own_ref), channel_id=1, source_target_pairs={{0,32},{32,0},{64,96},{96,64},{128,160},{160,128},{192,224},{224,1... | collective-permute-start | bytes 196616 | tf_op jit(solution)/shard_map/ppermute | solution.py:390
  51.9 4.6 %suffix_terms.1.m_ref = bf16[4,8,128,256]{3,2,1,0:T(8,128)(2,1)} custom-call(bf16[4,8,128,256]{3,2,1,0:T(8,128)(2,1)} %get-tuple-element.48.n_ref, bf16[4,8,128,256]{3,2,1,0:T(8,128)(2,1)} %get-tuple-element.49.t_ref, f32[6,128,128]{2,1,0:T(8,128)} %get-tuple-element.50.suf_ref), custom_call_target="tpu_custom_call" | custom-call | flops 805306368 | bytes 7340032 | tf_op jit(solution)/shard_map/suffix_terms/pallas_call | solution.py:443
  56.5 0.0 collective-permute-done.other_ref
  56.5 0.2 shard_map.46
  56.7 5.3 %all-to-all-done.1 = bf16[32,256,128]{2,1,0:T(8,128)(2,1)S(1)} async-done(((bf16[32,256,128]{2,1,0:T(8,128)(2,1)}), bf16[32,256,128]{2,1,0:T(8,128)(2,1)S(1)}, u32[]{:S(2)}, u32[]{:S(2)}) %all-to-all-start.1) | async-done | bytes 2097184 | tf_op jit(solution)/shard_map/all_to_all | solution.py:402
  62.0 2.2 %offset_total.1.own_ref = f32[128,128]{1,0:T(8,128)S(1)} custom-call(bf16[4,8,256,128]{3,2,1,0:T(8,128)(2,1)S(1)} %bitcast.17, bf16[4,8,128,256]{3,2,1,0:T(8,128)(2,1)} %suffix_terms.1.m_ref), custom_call_target="tpu_custom_call" | custom-call | flops 268435456 | bytes 3145728 | tf_op jit(solution)/shard_map/offset_total/pallas_call | solution.py:462
  64.1 1.7 %collective-permute-start.1 = (f32[128,128]{1,0:T(8,128)S(1)}, f32[128,128]{1,0:T(8,128)S(1)}, u32[]{:S(2)}, u32[]{:S(2)}) collective-permute-start(f32[128,128]{1,0:T(8,128)S(1)} %offset_total.1.own_ref), channel_id=1, source_target_pairs={{0,32},{32,0},{64,96},{96,64},{128,160},{160,128},{192,224},{224,1... | collective-permute-start | bytes 196616 | tf_op jit(solution)/shard_map/ppermute | solution.py:390
  65.9 3.0 %collective-permute-start.3 = (f32[128,128]{1,0:T(8,128)S(1)}, f32[128,128]{1,0:T(8,128)S(1)}, u32[]{:S(2)}, u32[]{:S(2)}) collective-permute-start(f32[128,128]{1,0:T(8,128)S(1)} %get-tuple-element.65.own_ref), channel_id=1, source_target_pairs={{0,64},{32,96},{64,0},{96,32},{128,192},{160,224},{192,128},{224,1... | collective-permute-start | bytes 196616 | tf_op jit(solution)/shard_map/ppermute | solution.py:390
  68.9 2.8 %scores.1.s_ref = bf16[4,8,128,256]{3,2,1,0:T(8,128)(2,1)} custom-call(bf16[4,8,256,128]{3,2,1,0:T(8,128)(2,1)S(1)} %bitcast.18, bf16[4,8,136,128]{3,2,1,0:T(8,128)(2,1)S(1)} %bitcast.23, f32[4,8,1,128]{3,2,1,0:T(1,128)} %get-tuple-element.55.c_ref), custom_call_target="tpu_custom_call" | custom-call | flops 134217728 | bytes 4194304 | tf_op jit(solution)/shard_map/scores/pallas_call | solution.py:474
  71.6 0.0 collective-permute-done.1.other_ref
  71.6 0.2 shard_map.47
  71.8 0.1 collective-permute-start.2
  71.9 0.0 collective-permute-done.3.other_ref
  71.9 0.2 shard_map.48
  72.1 3.5 %values_terms.2 = (f32[1,8,128,128]{3,2,1,0:T(8,128)}, f32[1,8,128,128]{3,2,1,0:T(8,128)}, f32[1,128,128]{2,1,0:T(8,128)}) custom-call(bf16[4,8,256,128]{3,2,1,0:T(8,128)(2,1)S(1)} %bitcast.19, bf16[4,8,128,256]{3,2,1,0:T(8,128)(2,1)} %get-tuple-element.61.xu_ref, bf16[4,8,128,256]{3,2,1,0:T(8,128)(2,1)} %get-tuple-element.48.n_ref, ...), custom_call_target="tpu_custom_call" | custom-call | flops 134217728 | bytes 3145728 | tf_op jit(solution)/shard_map/values_terms/pallas_call | solution.py:492
  75.6 0.8 collective-permute-done.2.other_ref
  76.4 0.2 shard_map.49
  76.6 4.8 %collective-permute-start.4 = (f32[128,128]{1,0:T(8,128)S(1)}, f32[128,128]{1,0:T(8,128)S(1)}, u32[]{:S(2)}, u32[]{:S(2)}) collective-permute-start(f32[128,128]{1,0:T(8,128)S(1)} %get-tuple-element.70), channel_id=1, source_target_pairs={{0,128},{32,160},{64,192},{96,224},{128,0},{160,32},{192,64},{224,... | collective-permute-start | bytes 196616 | tf_op jit(solution)/shard_map/ppermute | solution.py:390
  81.5 0.0 copy-start
  81.5 0.0 copy-start.1
  81.5 0.0 copy-start.2
  81.5 0.0 copy-start.3
  81.5 0.0 copy-start.4
  81.5 4.1 %values_terms.3 = (f32[3,8,128,128]{3,2,1,0:T(8,128)S(1)}, f32[3,8,128,128]{3,2,1,0:T(8,128)S(1)}, f32[3,128,128]{2,1,0:T(8,128)S(1)}) custom-call(bf16[4,8,256,128]{3,2,1,0:T(8,128)(2,1)S(1)} %bitcast.20, bf16[4,8,128,256]{3,2,1,0:T(8,128)(2,1)} %get-tuple-element.61.xu_ref, bf16[4,8,128,256]{3,2,1,0:T(8,128)(2,1)} %get-tuple-element.48.n_ref, ...), custom_call_target="tpu_custom_call" | custom-call | flops 402653184 | bytes 9437184 | tf_op jit(solution)/shard_map/values_terms/pallas_call | solution.py:492
  85.6 0.0 collective-permute-done.4.other_ref
  85.6 0.0 copy-done
  85.6 0.0 copy-done.1
  85.7 0.1 copy-done.2
  85.8 0.0 copy-done.3
  85.8 0.1 copy-done.4
  86.0 4.4 %mix_output.1 = bf16[4,8,128,128]{3,2,1,0:T(8,128)(2,1)S(1)} custom-call(s32[1]{0:T(128)} %bitcast.up_ref, f32[128,128]{1,0:T(8,128)S(1)} %collective-permute-done.4.other_ref, f32[128,128]{1,0:T(8,128)S(1)} %get-tuple-element.71.et_ref, f32[128,128]{1,0:T(8,128)S(1)} %get-tuple-element.72.eo_ref, f32[4,128,128]{2,1,0:T(8,128)} %get-tuple-element.73.pcum_ref, ...), custom_call_target="tpu_custom_call" | custom-call | flops 1610612736 | bytes 11534336 | tf_op jit(solution)/shard_map/mix_output/pallas_call | solution.py:520
  90.3 22.4 %all_to_all.15 = bf16[32,128,128]{2,1,0:T(8,128)(2,1)S(1)} all-to-all(bf16[32,128,128]{2,1,0:T(8,128)(2,1)S(1)} %bitcast.24), channel_id=1, replica_groups=mesh['z'=8,'x'=4,'y'=4,'core'=2] {'x','y','core'}, dimensions={0} | all-to-all | bytes 2097152 | tf_op jit(solution)/shard_map/all_to_all | solution.py:402
  112.7 1.6 %copy.16 = bf16[128,32,128]{2,1,0:T(8,128)(2,1)} copy(bf16[128,32,128]{2,0,1:T(8,128)(2,1)S(1)} %bitcast.26) | data formatting | bytes 2097152 | tf_op jit(solution)/shard_map/transpose | solution.py:539
Async XLA Ops:
  2.4 9.7 %copy-start.5 = (bf16[128,32,128]{2,1,0:T(8,128)(2,1)S(1)}, bf16[128,32,128]{2,1,0:T(8,128)(2,1)}, u32[]{:S(2)}) copy-start(bf16[128,32,128]{2,1,0:T(8,128)(2,1)} %param.4) | copy-start | bytes 3145732
  2.4 9.7 %copy-start.6 = (bf16[128,32,128]{2,1,0:T(8,128)(2,1)S(1)}, bf16[128,32,128]{2,1,0:T(8,128)(2,1)}, u32[]{:S(2)}) copy-start(bf16[128,32,128]{2,1,0:T(8,128)(2,1)} %param.6) | copy-start | bytes 3145732
  3.5 26.2 %all-to-all-start = ((bf16[32,136,128]{2,1,0:T(8,128)(2,1)}), bf16[32,136,128]{2,1,0:T(8,128)(2,1)S(1)}, u32[]{:S(2)}, u32[]{:S(2)}) async-start(bf16[32,136,128]{2,1,0:T(8,128)(2,1)} %fusion.1), calls=%async_computation | async-start | bytes 2228224 | tf_op jit(solution)/shard_map/all_to_all | solution.py:402
  29.7 32.2 %all-to-all-start.1 = ((bf16[32,256,128]{2,1,0:T(8,128)(2,1)}), bf16[32,256,128]{2,1,0:T(8,128)(2,1)S(1)}, u32[]{:S(2)}, u32[]{:S(2)}) async-start(bf16[32,256,128]{2,1,0:T(8,128)(2,1)} %pad_maximum_fusion), calls=%async_computation.1 | async-start | bytes 4194304 | tf_op jit(solution)/shard_map/all_to_all | solution.py:402
  50.1 6.4 %collective-permute-start = (f32[128,128]{1,0:T(8,128)S(1)}, f32[128,128]{1,0:T(8,128)S(1)}, u32[]{:S(2)}, u32[]{:S(2)}) collective-permute-start(f32[128,128]{1,0:T(8,128)S(1)} %get-tuple-element.46.own_ref), channel_id=1, source_target_pairs={{0,32},{32,0},{64,96},{96,64},{128,160},{160,128},{192,224},{224,1... | collective-permute-start | bytes 196616 | tf_op jit(solution)/shard_map/ppermute | solution.py:390
  64.1 7.5 %collective-permute-start.1 = (f32[128,128]{1,0:T(8,128)S(1)}, f32[128,128]{1,0:T(8,128)S(1)}, u32[]{:S(2)}, u32[]{:S(2)}) collective-permute-start(f32[128,128]{1,0:T(8,128)S(1)} %offset_total.1.own_ref), channel_id=1, source_target_pairs={{0,32},{32,0},{64,96},{96,64},{128,160},{160,128},{192,224},{224,1... | collective-permute-start | bytes 196616 | tf_op jit(solution)/shard_map/ppermute | solution.py:390
  65.9 6.1 %collective-permute-start.3 = (f32[128,128]{1,0:T(8,128)S(1)}, f32[128,128]{1,0:T(8,128)S(1)}, u32[]{:S(2)}, u32[]{:S(2)}) collective-permute-start(f32[128,128]{1,0:T(8,128)S(1)} %get-tuple-element.65.own_ref), channel_id=1, source_target_pairs={{0,64},{32,96},{64,0},{96,32},{128,192},{160,224},{192,128},{224,1... | collective-permute-start | bytes 196616 | tf_op jit(solution)/shard_map/ppermute | solution.py:390
  71.8 4.6 %collective-permute-start.2 = (f32[128,128]{1,0:T(8,128)S(1)}, f32[128,128]{1,0:T(8,128)S(1)}, u32[]{:S(2)}, u32[]{:S(2)}) collective-permute-start(f32[128,128]{1,0:T(8,128)S(1)} %get-tuple-element.60.own_ref), channel_id=1, source_target_pairs={{0,64},{32,96},{64,0},{96,32},{128,192},{160,224},{192,128},{224,1... | collective-permute-start | bytes 196616 | tf_op jit(solution)/shard_map/ppermute | solution.py:390
  76.6 9.0 %collective-permute-start.4 = (f32[128,128]{1,0:T(8,128)S(1)}, f32[128,128]{1,0:T(8,128)S(1)}, u32[]{:S(2)}, u32[]{:S(2)}) collective-permute-start(f32[128,128]{1,0:T(8,128)S(1)} %get-tuple-element.70), channel_id=1, source_target_pairs={{0,128},{32,160},{64,192},{96,224},{128,0},{160,32},{192,64},{224,... | collective-permute-start | bytes 196616 | tf_op jit(solution)/shard_map/ppermute | solution.py:390
  81.5 4.2 %copy-start = (bf16[4,8,128,256]{3,2,1,0:T(8,128)(2,1)S(1)}, bf16[4,8,128,256]{3,2,1,0:T(8,128)(2,1)}, u32[]{:S(2)}) copy-start(bf16[4,8,128,256]{3,2,1,0:T(8,128)(2,1)} %scores.1.s_ref) | copy-start | bytes 6291460
  81.5 4.2 %copy-start.1 = (bf16[4,8,128,256]{3,2,1,0:T(8,128)(2,1)S(1)}, bf16[4,8,128,256]{3,2,1,0:T(8,128)(2,1)}, u32[]{:S(2)}) copy-start(bf16[4,8,128,256]{3,2,1,0:T(8,128)(2,1)} %get-tuple-element.77.yw_ref) | copy-start | bytes 6291460
  81.5 4.3 %copy-start.2 = (bf16[4,8,128,256]{3,2,1,0:T(8,128)(2,1)S(1)}, bf16[4,8,128,256]{3,2,1,0:T(8,128)(2,1)}, u32[]{:S(2)}) copy-start(bf16[4,8,128,256]{3,2,1,0:T(8,128)(2,1)} %get-tuple-element.78.p_ref) | copy-start | bytes 6291460
  81.5 4.3 %copy-start.3 = (f32[1,8,128,128]{3,2,1,0:T(8,128)S(1)}, f32[1,8,128,128]{3,2,1,0:T(8,128)}, u32[]{:S(2)}) copy-start(f32[1,8,128,128]{3,2,1,0:T(8,128)} %get-tuple-element.80.yub_ref) | copy-start | bytes 1572868
  81.5 4.5 %copy-start.4 = (f32[1,8,128,128]{3,2,1,0:T(8,128)S(1)}, f32[1,8,128,128]{3,2,1,0:T(8,128)}, u32[]{:S(2)}) copy-start(f32[1,8,128,128]{3,2,1,0:T(8,128)} %get-tuple-element.82.ob_ref) | copy-start | bytes 1572868

commit v4 on v3

--- a/solution.py
+++ b/solution.py
@@ -404,7 +404,7 @@
     def by_super(array):
         return array.reshape((SUPER, STEPS) + array.shape[1:])
 
-    gates = jnp.pad(beta.T[:, None, :], ((0, 0), (0, PACK - SPAN - 1), (0, 0)))
+    gates = jnp.broadcast_to(beta.T[:, None, :], (beta.shape[1], PACK - SPAN, beta.shape[0]))
     packed = jnp.concatenate([heads_first(keys), gates], axis=1)
     mixed = jnp.concatenate([heads_first(value), heads_first(query)], axis=1)
     kp = to_heads(packed)
@@ -510,7 +510,7 @@
     off4, eo2 = small(quad_offset_kernel, 2, up2, off2, other, tup2, et1, eo1)
     vq, off4 = lax.optimization_barrier((vq, off4))
     yua, oa, end = values_part(SUPER - 1, 0, vq, False)
-    other = exchange(off4, 4, depth)
+    other = exchange(off4, 7, depth)
 
     def all_of(count, *shape, place=0):
         return pl.BlockSpec((count, STEPS) + shape, lambda b: (0, 0, place, 0))

time: 115 us -> 113 us (0.983)
  starting transfers between devices: 23.9 us -> 22.5 us
    ppermute x5, starting transfers between devices: 11.4 us -> 10 us  [exchange(): return lax.ppermute(x, 'z', [(i, i ^ distance) for i in range(size)])]
    unnamed x16 -> x17, local copies, waits for them, and re-layouts: 2.68 us -> 1.99 us
where the time goes in v4:
time: 113 us; the launch traced here: 112 us
  Pallas kernels  38.7 us (34%)
  starting transfers between devices  22.5 us (20%)
  blocking collectives  22.4 us (20%)
  waiting for transfers between devices  21.3 us (19%)
  local copies, waits for them, and re-layouts  4.47 us (4%)
  other arithmetic  2.69 us (2%)
    all_to_all x1, blocking collectives, to_heads(): return lax.all_to_all(array, GROUP, split_axis=0, concat_axis=0, tiled=True)  22.4 us
    all_to_all x2, waiting for transfers between devices, to_heads(): return lax.all_to_all(array, GROUP, split_axis=0, concat_axis=0, tiled=True)  20.5 us
    pallas_call x1, Pallas kernels, shards(): pl.pallas_call(keys_kernel, grid=(steps,), in_specs=[block(PACK, DIM)], o...  16.5 us
    all_to_all x2, starting transfers between devices, to_heads(): return lax.all_to_all(array, GROUP, split_axis=0, concat_axis=0, tiled=True)  12.5 us
    ppermute x5, starting transfers between devices, exchange(): return lax.ppermute(x, 'z', [(i, i ^ distance) for i in range(size)])  10 us
    pallas_call x2, Pallas kernels, values_part(): pl.pallas_call(values_kernel, grid=(STEPS // LONG,), in_specs=[pl.BlockSp...  7.62 us
    pallas_call x1, Pallas kernels, shards(): pl.pallas_call(suffix_kernel, grid=(2,), in_specs=[back_block, back_block...  4.63 us
    pallas_call x1, Pallas kernels, shards(): pl.pallas_call(output_kernel, grid=(1,), in_specs=[SMEM, whole(DIM, DIM),...  4.37 us
  transfers between devices with their start and end apart: 7, of which 3 were waited for; matrix products, arithmetic and copies ran while one was open for 2% of the time, Pallas kernels for 28%

profile of v4, /device:TPU:1, one launch (start us, length us, event | category | flops | bytes accessed | tf_op | source)
XLA Modules:
  0.0 112.3 jit_solution(12715014407091863414)
XLA Ops:
  0.0 0.0 copy-start.7
  0.0 1.6 %copy.15 = bf16[128,32,128]{2,0,1:T(8,128)(2,1)S(1)} copy(bf16[128,32,128]{2,1,0:T(8,128)(2,1)} %param.5) | data formatting | bytes 2097152 | tf_op args[1]
  1.6 0.0 copy-done.7
  1.7 0.0 copy-start.5
  1.7 0.0 copy-start.6
  1.7 1.1 pad_maximum_fusion.1
  2.8 8.6 %all-to-all-start = ((bf16[32,136,128]{2,1,0:T(8,128)(2,1)}), bf16[32,136,128]{2,1,0:T(8,128)(2,1)S(1)}, u32[]{:S(2)}, u32[]{:S(2)}) async-start(bf16[32,136,128]{2,1,0:T(8,128)(2,1)} %pad_maximum_fusion.1), calls=%async_computation | async-start | bytes 2228224 | tf_op jit(solution)/shard_map/all_to_all | solution.py:402
  11.4 0.0 copy-done.5
  11.4 0.0 copy-done.6
  11.4 0.8 copy_bitcast_fusion.1
  12.3 1.6 %pad_maximum_fusion = bf16[32,256,128]{2,1,0:T(8,128)(2,1)} fusion(bf16[32,128,128]{2,1,0:T(8,128)(2,1)S(1)} %get-tuple-element.83, bf16[32,128,128]{2,1,0:T(8,128)(2,1)S(1)} %get-tuple-element.84), kind=kLoop, calls=%fused_computation | loop fusion | flops 4194304 | bytes 4194304 | tf_op jit(solution)/shard_map/concatenate | solution.py:409
  13.8 15.2 %all-to-all-done = bf16[32,136,128]{2,1,0:T(8,128)(2,1)S(1)} async-done(((bf16[32,136,128]{2,1,0:T(8,128)(2,1)}), bf16[32,136,128]{2,1,0:T(8,128)(2,1)S(1)}, u32[]{:S(2)}, u32[]{:S(2)}) %all-to-all-start) | async-done | bytes 1114144 | tf_op jit(solution)/shard_map/all_to_all | solution.py:402
  29.1 3.9 %all-to-all-start.1 = ((bf16[32,256,128]{2,1,0:T(8,128)(2,1)}), bf16[32,256,128]{2,1,0:T(8,128)(2,1)S(1)}, u32[]{:S(2)}, u32[]{:S(2)}) async-start(bf16[32,256,128]{2,1,0:T(8,128)(2,1)} %pad_maximum_fusion), calls=%async_computation.1 | async-start | bytes 4194304 | tf_op jit(solution)/shard_map/all_to_all | solution.py:402
  33.0 16.5 %keys_terms.1 = (bf16[4,8,128,256]{3,2,1,0:T(8,128)(2,1)}, bf16[4,8,128,256]{3,2,1,0:T(8,128)(2,1)}, bf16[4,8,128,256]{3,2,1,0:T(8,128)(2,1)}, bf16[4,8,128,256]...) custom-call(bf16[4,8,136,128]{3,2,1,0:T(8,128)(2,1)S(1)} %bitcast.20), custom_call_target="tpu_custom_call" | custom-call | flops 6308233216 | bytes 11534336 | tf_op jit(solution)/shard_map/keys_terms/pallas_call | solution.py:420
  49.5 1.7 %collective-permute-start = (f32[128,128]{1,0:T(8,128)S(1)}, f32[128,128]{1,0:T(8,128)S(1)}, u32[]{:S(2)}, u32[]{:S(2)}) collective-permute-start(f32[128,128]{1,0:T(8,128)S(1)} %get-tuple-element.46.own_ref), channel_id=1, source_target_pairs={{0,32},{32,0},{64,96},{96,64},{128,160},{160,128},{192,224},{224,1... | collective-permute-start | bytes 196616 | tf_op jit(solution)/shard_map/ppermute | solution.py:390
  51.2 4.6 %suffix_terms.1.m_ref = bf16[4,8,128,256]{3,2,1,0:T(8,128)(2,1)} custom-call(bf16[4,8,128,256]{3,2,1,0:T(8,128)(2,1)} %get-tuple-element.48.n_ref, bf16[4,8,128,256]{3,2,1,0:T(8,128)(2,1)} %get-tuple-element.49.t_ref, f32[6,128,128]{2,1,0:T(8,128)} %get-tuple-element.50.suf_ref), custom_call_target="tpu_custom_call" | custom-call | flops 805306368 | bytes 7340032 | tf_op jit(solution)/shard_map/suffix_terms/pallas_call | solution.py:443
  55.8 0.0 collective-permute-done.other_ref
  55.8 0.2 shard_map.46
  56.0 5.3 %all-to-all-done.1 = bf16[32,256,128]{2,1,0:T(8,128)(2,1)S(1)} async-done(((bf16[32,256,128]{2,1,0:T(8,128)(2,1)}), bf16[32,256,128]{2,1,0:T(8,128)(2,1)S(1)}, u32[]{:S(2)}, u32[]{:S(2)}) %all-to-all-start.1) | async-done | bytes 2097184 | tf_op jit(solution)/shard_map/all_to_all | solution.py:402
  61.3 2.2 %offset_total.1.own_ref = f32[128,128]{1,0:T(8,128)S(1)} custom-call(bf16[4,8,256,128]{3,2,1,0:T(8,128)(2,1)S(1)} %bitcast.15, bf16[4,8,128,256]{3,2,1,0:T(8,128)(2,1)} %suffix_terms.1.m_ref), custom_call_target="tpu_custom_call" | custom-call | flops 268435456 | bytes 3145728 | tf_op jit(solution)/shard_map/offset_total/pallas_call | solution.py:462
  63.5 1.7 %collective-permute-start.1 = (f32[128,128]{1,0:T(8,128)S(1)}, f32[128,128]{1,0:T(8,128)S(1)}, u32[]{:S(2)}, u32[]{:S(2)}) collective-permute-start(f32[128,128]{1,0:T(8,128)S(1)} %offset_total.1.own_ref), channel_id=1, source_target_pairs={{0,32},{32,0},{64,96},{96,64},{128,160},{160,128},{192,224},{224,1... | collective-permute-start | bytes 196616 | tf_op jit(solution)/shard_map/ppermute | solution.py:390
  65.2 3.0 %collective-permute-start.3 = (f32[128,128]{1,0:T(8,128)S(1)}, f32[128,128]{1,0:T(8,128)S(1)}, u32[]{:S(2)}, u32[]{:S(2)}) collective-permute-start(f32[128,128]{1,0:T(8,128)S(1)} %get-tuple-element.65.own_ref), channel_id=1, source_target_pairs={{0,64},{32,96},{64,0},{96,32},{128,192},{160,224},{192,128},{224,1... | collective-permute-start | bytes 196616 | tf_op jit(solution)/shard_map/ppermute | solution.py:390
  68.2 2.8 %scores.1.s_ref = bf16[4,8,128,256]{3,2,1,0:T(8,128)(2,1)} custom-call(bf16[4,8,256,128]{3,2,1,0:T(8,128)(2,1)S(1)} %bitcast.16, bf16[4,8,136,128]{3,2,1,0:T(8,128)(2,1)S(1)} %bitcast.21, f32[4,8,1,128]{3,2,1,0:T(1,128)} %get-tuple-element.55.c_ref), custom_call_target="tpu_custom_call" | custom-call | flops 134217728 | bytes 4194304 | tf_op jit(solution)/shard_map/scores/pallas_call | solution.py:474
  70.9 0.0 collective-permute-done.1.other_ref
  70.9 0.2 shard_map.47
  71.1 0.1 collective-permute-start.2
  71.2 0.0 collective-permute-done.3.other_ref
  71.2 0.2 shard_map.48
  71.4 3.5 %values_terms.2 = (f32[1,8,128,128]{3,2,1,0:T(8,128)}, f32[1,8,128,128]{3,2,1,0:T(8,128)}, f32[1,128,128]{2,1,0:T(8,128)}) custom-call(bf16[4,8,256,128]{3,2,1,0:T(8,128)(2,1)S(1)} %bitcast.17, bf16[4,8,128,256]{3,2,1,0:T(8,128)(2,1)} %get-tuple-element.61.xu_ref, bf16[4,8,128,256]{3,2,1,0:T(8,128)(2,1)} %get-tuple-element.48.n_ref, ...), custom_call_target="tpu_custom_call" | custom-call | flops 134217728 | bytes 3145728 | tf_op jit(solution)/shard_map/values_terms/pallas_call | solution.py:492
  74.9 0.8 collective-permute-done.2.other_ref
  75.7 0.2 shard_map.49
  76.0 3.5 %collective-permute-start.4 = (f32[128,128]{1,0:T(8,128)S(1)}, f32[128,128]{1,0:T(8,128)S(1)}, u32[]{:S(2)}, u32[]{:S(2)}) collective-permute-start(f32[128,128]{1,0:T(8,128)S(1)} %get-tuple-element.70), channel_id=1, source_target_pairs={{0,224},{32,192},{64,160},{96,128},{128,96},{160,64},{192,32},{224... | collective-permute-start | bytes 196616 | tf_op jit(solution)/shard_map/ppermute | solution.py:390
  79.5 0.0 copy-start
  79.5 0.0 copy-start.1
  79.5 0.0 copy-start.2
  79.5 0.0 copy-start.3
  79.5 0.0 copy-start.4
  79.5 4.1 %values_terms.3 = (f32[3,8,128,128]{3,2,1,0:T(8,128)S(1)}, f32[3,8,128,128]{3,2,1,0:T(8,128)S(1)}, f32[3,128,128]{2,1,0:T(8,128)S(1)}) custom-call(bf16[4,8,256,128]{3,2,1,0:T(8,128)(2,1)S(1)} %bitcast.18, bf16[4,8,128,256]{3,2,1,0:T(8,128)(2,1)} %get-tuple-element.61.xu_ref, bf16[4,8,128,256]{3,2,1,0:T(8,128)(2,1)} %get-tuple-element.48.n_ref, ...), custom_call_target="tpu_custom_call" | custom-call | flops 402653184 | bytes 9437184 | tf_op jit(solution)/shard_map/values_terms/pallas_call | solution.py:492
  83.6 0.0 collective-permute-done.4.other_ref
  83.6 0.0 copy-done
  83.6 0.0 copy-done.1
  83.6 0.1 copy-done.2
  83.7 0.0 copy-done.3
  83.8 0.1 copy-done.4
  83.9 4.4 %mix_output.1 = bf16[4,8,128,128]{3,2,1,0:T(8,128)(2,1)S(1)} custom-call(s32[1]{0:T(128)} %bitcast.up_ref, f32[128,128]{1,0:T(8,128)S(1)} %collective-permute-done.4.other_ref, f32[128,128]{1,0:T(8,128)S(1)} %get-tuple-element.71.et_ref, f32[128,128]{1,0:T(8,128)S(1)} %get-tuple-element.72.eo_ref, f32[4,128,128]{2,1,0:T(8,128)} %get-tuple-element.73.pcum_ref, ...), custom_call_target="tpu_custom_call" | custom-call | flops 1610612736 | bytes 11534336 | tf_op jit(solution)/shard_map/mix_output/pallas_call | solution.py:520
  88.3 22.4 %all_to_all.15 = bf16[32,128,128]{2,1,0:T(8,128)(2,1)S(1)} all-to-all(bf16[32,128,128]{2,1,0:T(8,128)(2,1)S(1)} %bitcast.22), channel_id=1, replica_groups=mesh['z'=8,'x'=4,'y'=4,'core'=2] {'x','y','core'}, dimensions={0} | all-to-all | bytes 2097152 | tf_op jit(solution)/shard_map/all_to_all | solution.py:402
  110.7 1.6 %copy.11 = bf16[128,32,128]{2,1,0:T(8,128)(2,1)} copy(bf16[128,32,128]{2,0,1:T(8,128)(2,1)S(1)} %bitcast.24) | data formatting | bytes 2097152 | tf_op jit(solution)/shard_map/transpose | solution.py:539
  (1 shorter events, 0.0 us)
Async XLA Ops:
  0.0 1.7 %copy-start.7 = (bf16[128,32]{0,1:T(8,128)(2,1)S(1)}, bf16[128,32]{0,1:T(8,128)(2,1)}, u32[]{:S(2)}) copy-start(bf16[128,32]{0,1:T(8,128)(2,1)} %param.7) | copy-start | bytes 24580
  1.7 9.7 %copy-start.5 = (bf16[128,32,128]{2,1,0:T(8,128)(2,1)S(1)}, bf16[128,32,128]{2,1,0:T(8,128)(2,1)}, u32[]{:S(2)}) copy-start(bf16[128,32,128]{2,1,0:T(8,128)(2,1)} %param.4) | copy-start | bytes 3145732
  1.7 9.7 %copy-start.6 = (bf16[128,32,128]{2,1,0:T(8,128)(2,1)S(1)}, bf16[128,32,128]{2,1,0:T(8,128)(2,1)}, u32[]{:S(2)}) copy-start(bf16[128,32,128]{2,1,0:T(8,128)(2,1)} %param.6) | copy-start | bytes 3145732
  2.8 26.2 %all-to-all-start = ((bf16[32,136,128]{2,1,0:T(8,128)(2,1)}), bf16[32,136,128]{2,1,0:T(8,128)(2,1)S(1)}, u32[]{:S(2)}, u32[]{:S(2)}) async-start(bf16[32,136,128]{2,1,0:T(8,128)(2,1)} %pad_maximum_fusion.1), calls=%async_computation | async-start | bytes 2228224 | tf_op jit(solution)/shard_map/all_to_all | solution.py:402
  29.1 32.2 %all-to-all-start.1 = ((bf16[32,256,128]{2,1,0:T(8,128)(2,1)}), bf16[32,256,128]{2,1,0:T(8,128)(2,1)S(1)}, u32[]{:S(2)}, u32[]{:S(2)}) async-start(bf16[32,256,128]{2,1,0:T(8,128)(2,1)} %pad_maximum_fusion), calls=%async_computation.1 | async-start | bytes 4194304 | tf_op jit(solution)/shard_map/all_to_all | solution.py:402
  49.5 6.4 %collective-permute-start = (f32[128,128]{1,0:T(8,128)S(1)}, f32[128,128]{1,0:T(8,128)S(1)}, u32[]{:S(2)}, u32[]{:S(2)}) collective-permute-start(f32[128,128]{1,0:T(8,128)S(1)} %get-tuple-element.46.own_ref), channel_id=1, source_target_pairs={{0,32},{32,0},{64,96},{96,64},{128,160},{160,128},{192,224},{224,1... | collective-permute-start | bytes 196616 | tf_op jit(solution)/shard_map/ppermute | solution.py:390
  63.5 7.5 %collective-permute-start.1 = (f32[128,128]{1,0:T(8,128)S(1)}, f32[128,128]{1,0:T(8,128)S(1)}, u32[]{:S(2)}, u32[]{:S(2)}) collective-permute-start(f32[128,128]{1,0:T(8,128)S(1)} %offset_total.1.own_ref), channel_id=1, source_target_pairs={{0,32},{32,0},{64,96},{96,64},{128,160},{160,128},{192,224},{224,1... | collective-permute-start | bytes 196616 | tf_op jit(solution)/shard_map/ppermute | solution.py:390
  65.2 6.0 %collective-permute-start.3 = (f32[128,128]{1,0:T(8,128)S(1)}, f32[128,128]{1,0:T(8,128)S(1)}, u32[]{:S(2)}, u32[]{:S(2)}) collective-permute-start(f32[128,128]{1,0:T(8,128)S(1)} %get-tuple-element.65.own_ref), channel_id=1, source_target_pairs={{0,64},{32,96},{64,0},{96,32},{128,192},{160,224},{192,128},{224,1... | collective-permute-start | bytes 196616 | tf_op jit(solution)/shard_map/ppermute | solution.py:390
  71.1 4.6 %collective-permute-start.2 = (f32[128,128]{1,0:T(8,128)S(1)}, f32[128,128]{1,0:T(8,128)S(1)}, u32[]{:S(2)}, u32[]{:S(2)}) collective-permute-start(f32[128,128]{1,0:T(8,128)S(1)} %get-tuple-element.60.own_ref), channel_id=1, source_target_pairs={{0,64},{32,96},{64,0},{96,32},{128,192},{160,224},{192,128},{224,1... | collective-permute-start | bytes 196616 | tf_op jit(solution)/shard_map/ppermute | solution.py:390
  76.0 7.6 %collective-permute-start.4 = (f32[128,128]{1,0:T(8,128)S(1)}, f32[128,128]{1,0:T(8,128)S(1)}, u32[]{:S(2)}, u32[]{:S(2)}) collective-permute-start(f32[128,128]{1,0:T(8,128)S(1)} %get-tuple-element.70), channel_id=1, source_target_pairs={{0,224},{32,192},{64,160},{96,128},{128,96},{160,64},{192,32},{224... | collective-permute-start | bytes 196616 | tf_op jit(solution)/shard_map/ppermute | solution.py:390
  79.5 4.1 %copy-start = (bf16[4,8,128,256]{3,2,1,0:T(8,128)(2,1)S(1)}, bf16[4,8,128,256]{3,2,1,0:T(8,128)(2,1)}, u32[]{:S(2)}) copy-start(bf16[4,8,128,256]{3,2,1,0:T(8,128)(2,1)} %scores.1.s_ref) | copy-start | bytes 6291460
  79.5 4.1 %copy-start.1 = (bf16[4,8,128,256]{3,2,1,0:T(8,128)(2,1)S(1)}, bf16[4,8,128,256]{3,2,1,0:T(8,128)(2,1)}, u32[]{:S(2)}) copy-start(bf16[4,8,128,256]{3,2,1,0:T(8,128)(2,1)} %get-tuple-element.77.yw_ref) | copy-start | bytes 6291460
  79.5 4.3 %copy-start.2 = (bf16[4,8,128,256]{3,2,1,0:T(8,128)(2,1)S(1)}, bf16[4,8,128,256]{3,2,1,0:T(8,128)(2,1)}, u32[]{:S(2)}) copy-start(bf16[4,8,128,256]{3,2,1,0:T(8,128)(2,1)} %get-tuple-element.78.p_ref) | copy-start | bytes 6291460
  79.5 4.3 %copy-start.3 = (f32[1,8,128,128]{3,2,1,0:T(8,128)S(1)}, f32[1,8,128,128]{3,2,1,0:T(8,128)}, u32[]{:S(2)}) copy-start(f32[1,8,128,128]{3,2,1,0:T(8,128)} %get-tuple-element.80.yub_ref) | copy-start | bytes 1572868
  79.5 4.5 %copy-start.4 = (f32[1,8,128,128]{3,2,1,0:T(8,128)S(1)}, f32[1,8,128,128]{3,2,1,0:T(8,128)}, u32[]{:S(2)}) copy-start(f32[1,8,128,128]{3,2,1,0:T(8,128)} %get-tuple-element.82.ob_ref) | copy-start | bytes 1572868
